TPU v7x, 128 devices: a whole 4x4x4 slice. The times are simulated.
128 devices in a mesh: row: 16 (over y, z), col: 8 (over x, core).
Axes of the slice: x: 4, y: 4, z: 4, core: 2. Of those that a mesh axis runs over, the one named last changes fastest.
Arguments:
- child_parent: int32 [16384], P(('row', 'col')), may hold values from 0 to 4095, as said below
- prefix_len: int32 [16384], P(('row', 'col')), may hold values from 1 to 40
- child_delta: bfloat16 [16384, 3584], P(('row', 'col')), may hold values from -6 to 6
- parent_hidden: bfloat16 [4096, 3584], P(('row', 'col')), may hold values from -6 to 6
- parent_cache: bfloat16 [4096, 2, 2, 128, 128], P(('row', 'col')), may hold values from -720 to 720
- prefix_cache: bfloat16 [128, 2, 2, 5120, 128], P(('row', 'col')), may hold values from -720 to 720
- norm_gain: float32 [3584], replicated, may hold values from 0.1 to 1.9
- w_query: bfloat16 [3584, 1792], replicated, may hold values from -0.09375 to 0.09375
- w_kv: bfloat16 [3584, 512], replicated, may hold values from -0.09375 to 0.09375
Outputs:
- context: bfloat16 [16384, 1792], P(('row', 'col'))
- child_kv: bfloat16 [16384, 512], P(('row', 'col'))
Inputs may be any that keep to these rules, and one draw needn't show every extreme that they name: `child_parent`: each device's 128 children name exactly 16 parents held in each column of devices; the children of any one row of devices name exactly 8 parents held by any one device; one device's children name at most 2 parents held by one device, and exactly 2 for some pairs. Parent p is held by device p // 32, device index = row index * 8 + column index.
All inputs are finite; a program needn't handle non-finite values.
Results may differ from a plain program's by a relative error of at most 0.0085.
The roundings to bfloat16 on the way count: a program that leaves them out, or rounds other values in their place, can miss the bound.
Values may be sent and summed in bfloat16 or wider, within the bound.
A program may use at most 256 MiB of HBM per device.

v0:
```python
import math

import jax
import jax.numpy as jnp
from jax import lax
from jax.sharding import PartitionSpec as P

EPSILON = 1e-06


def side_by_side(arrays, axis, split_dim, concat_dim, along):
    widths = [a.shape[along] for a in arrays]
    both = jnp.concatenate(arrays, axis=along)
    result = lax.all_to_all(both, axis, split_axis=split_dim, concat_axis=concat_dim, tiled=True)
    return tuple(jnp.split(result, [sum(widths[:k]) for k in range(1, len(widths))], axis=along))


def project_rows(parent_rows, delta_rows, norm_gain, w_query, w_kv):
    widened = parent_rows.astype(jnp.float32) + delta_rows.astype(jnp.float32)
    inverse = lax.rsqrt(jnp.mean(widened * widened, axis=-1, keepdims=True) + EPSILON)
    normed = (widened * inverse * norm_gain).astype(jnp.bfloat16)
    queries = jnp.dot(normed, w_query, preferred_element_type=jnp.float32).astype(jnp.bfloat16)
    new_kv = jnp.dot(normed, w_kv, preferred_element_type=jnp.float32).astype(jnp.bfloat16)
    return (queries, new_kv)


def prefix_scores(grouped, block_counts, prefix_rows, block_tokens, scale_factor):
    score_pre = (
        jnp.einsum("chgd,hld->hcgl", grouped, prefix_rows[0], preferred_element_type=jnp.float32)
        * scale_factor
    )
    key_positions = jnp.arange(prefix_rows.shape[2], dtype=jnp.int32)
    limits = block_counts * block_tokens
    in_prefix = key_positions[None, None, None, :] < limits[None, :, None, None]
    return jnp.where(in_prefix, score_pre, -jnp.inf)


def pick_slots(member, rank_grid, values, slot_count):
    wanted = jnp.arange(slot_count, dtype=jnp.int32)
    match_mask = member[..., None, :] & (rank_grid[..., None, :] == wanted[:, None])
    return jnp.sum(jnp.where(match_mask, values[..., None, :], 0), axis=-1)


def direct_layout(
    whole_source, whole_local, my_source, my_device, device_count, per_device, capacity
):
    positions = jnp.arange(per_device, dtype=jnp.int32)
    source_grid = whole_source.reshape(device_count, per_device)
    local_grid = whole_local.reshape(device_count, per_device)
    member = source_grid == my_device
    rank_grid = jnp.cumsum(member.astype(jnp.int32), axis=1) - 1
    send_ids = pick_slots(member, rank_grid, local_grid, capacity)
    earlier = (my_source[None, :] == my_source[:, None]) & (positions[None, :] < positions[:, None])
    my_rank = jnp.sum(earlier.astype(jnp.int32), axis=1)
    return (send_ids, my_source * capacity + my_rank)


def heads_to_rows(stat, child_count):
    return jnp.transpose(stat[..., 0], (1, 0, 2)).reshape(child_count, -1)


def rows_to_heads(stat, child_count, kv_heads):
    return jnp.transpose(stat.reshape(child_count, kv_heads, -1), (1, 0, 2))[..., None]


def local(
    child_parent,
    prefix_len,
    child_delta,
    parent_hidden,
    parent_cache,
    prefix_cache,
    norm_gain,
    w_query,
    w_kv,
):
    row_count = lax.axis_size("row")
    col_count = lax.axis_size("col")
    device_count = row_count * col_count
    my_row = lax.axis_index("row")
    my_col = lax.axis_index("col")
    my_device = my_row * col_count + my_col
    per_device = child_parent.shape[0]
    parent_count = parent_hidden.shape[0]
    whole_map = lax.all_gather(child_parent, ("row", "col"), axis=0, tiled=True)
    whole_source = whole_map // parent_count
    whole_local = whole_map % parent_count
    my_source = child_parent // parent_count
    capacity = 2 * ((per_device // (2 * col_count) + row_count - 1) // row_count)
    send_ids, flat_index = direct_layout(
        whole_source, whole_local, my_source, my_device, device_count, per_device, capacity
    )
    arrived_hidden = lax.all_to_all(
        parent_hidden[send_ids], ("row", "col"), split_axis=0, concat_axis=0, tiled=True
    )
    hidden_rows = arrived_hidden.reshape(-1, arrived_hidden.shape[-1])[flat_index]
    queries, new_kv = project_rows(hidden_rows, child_delta, norm_gain, w_query, w_kv)
    prefix_rows = prefix_cache[0]
    kv_heads = prefix_rows.shape[1]
    head_dim = prefix_rows.shape[-1]
    block_tokens = parent_cache.shape[3]
    scale_factor = 1.0 / math.sqrt(head_dim)
    grouped = queries.reshape(per_device, kv_heads, -1, head_dim)
    score_pre = prefix_scores(grouped, prefix_len, prefix_rows, block_tokens, scale_factor)
    top_pre = jnp.max(score_pre, axis=-1, keepdims=True)
    sum_pre = jnp.sum(jnp.exp(score_pre - top_pre), axis=-1, keepdims=True)
    slot_total = device_count * capacity
    query_box = jnp.zeros((slot_total, queries.shape[1]), jnp.bfloat16).at[flat_index].set(queries)
    top_box = (
        jnp.zeros((slot_total, queries.shape[1] // head_dim), jnp.float32)
        .at[flat_index]
        .set(heads_to_rows(top_pre, per_device))
    )
    sum_box = (
        jnp.zeros((slot_total, queries.shape[1] // head_dim), jnp.float32)
        .at[flat_index]
        .set(heads_to_rows(sum_pre, per_device))
    )
    far_query, far_top, far_sum = (
        lax.all_to_all(
            query_box.reshape(device_count, capacity, -1).astype(jnp.float32),
            ("row", "col"),
            split_axis=0,
            concat_axis=0,
            tiled=True,
        ).astype(jnp.bfloat16),
        lax.all_to_all(
            top_box.reshape(device_count, capacity, -1),
            ("row", "col"),
            split_axis=0,
            concat_axis=0,
            tiled=True,
        ),
        lax.all_to_all(
            sum_box.reshape(device_count, capacity, -1),
            ("row", "col"),
            split_axis=0,
            concat_axis=0,
            tiled=True,
        ),
    )
    own_blocks = parent_cache[send_ids.reshape(-1)]
    item_query = far_query.reshape(slot_total, kv_heads, -1, head_dim)
    score_par = (
        jnp.einsum(
            "chgd,chtd->hcgt", item_query, own_blocks[:, 0], preferred_element_type=jnp.float32
        )
        * scale_factor
    )
    remote_top = rows_to_heads(far_top, slot_total, kv_heads)
    remote_sum = rows_to_heads(far_sum, slot_total, kv_heads)
    joint_top = jnp.maximum(remote_top, jnp.max(score_par, axis=-1, keepdims=True))
    exp_par = jnp.exp(score_par - joint_top)
    joint_sum = remote_sum * jnp.exp(remote_top - joint_top) + jnp.sum(
        exp_par, axis=-1, keepdims=True
    )
    weight_par = (exp_par / joint_sum).astype(jnp.bfloat16)
    share = jnp.einsum(
        "hcgt,chtd->chgd", weight_par, own_blocks[:, 1], preferred_element_type=jnp.float32
    )
    back_share, back_top, back_sum = side_by_side(
        (
            share.reshape(device_count, capacity, -1),
            heads_to_rows(joint_top, slot_total).reshape(device_count, capacity, -1),
            heads_to_rows(joint_sum, slot_total).reshape(device_count, capacity, -1),
        ),
        ("row", "col"),
        0,
        0,
        2,
    )
    child_share = back_share.reshape(slot_total, -1)[flat_index]
    child_top = rows_to_heads(back_top.reshape(slot_total, -1)[flat_index], per_device, kv_heads)
    child_sum = rows_to_heads(back_sum.reshape(slot_total, -1)[flat_index], per_device, kv_heads)
    weight_pre = (jnp.exp(score_pre - child_top) / child_sum).astype(jnp.bfloat16)
    context = jnp.einsum(
        "hcgl,hld->chgd", weight_pre, prefix_rows[1], preferred_element_type=jnp.float32
    )
    context = context + child_share.reshape(context.shape)
    return (context.reshape(per_device, -1).astype(jnp.bfloat16), new_kv)


def solution(mesh):
    return jax.shard_map(
        local,
        mesh=mesh,
        in_specs=(
            P(("row", "col")),
            P(("row", "col")),
            P(("row", "col"), None),
            P(("row", "col"), None),
            P(("row", "col"), None, None, None, None),
            P(("row", "col"), None, None, None, None),
            P(),
            P(),
            P(),
        ),
        out_specs=(P(("row", "col"), None), P(("row", "col"), None)),
        check_vma=False,
    )
```

profile of v0, /device:TPU:0, one launch (start us, length us, event | category | flops | bytes accessed | tf_op | source)
XLA Modules:
  0.0 276.2 jit_solution(15527719592834599393)
XLA Ops:
  0.7 33.3 %all-gather = s32[128,1,128]{2,1,0:T(1,128)S(1)} all-gather(s32[1,1,128]{2,1,0:T(1,128)} %bitcast.107), channel_id=1, replica_groups=mesh['row'=16,'col'=8] {'row','col'}, dimensions={0}, use_global_device_ids=true | all-gather | bytes 66048 | tf_op jit(solution)/shard_map/all_gather | solution.py:85
  34.1 0.2 reduce_window_sum.11
  34.8 1.7 gather_fusion
  36.6 1.7 reshape.190
  38.2 8.3 %all-to-all-start = ((bf16[128,2,3584]{2,1,0:T(2,128)(2,1)}), bf16[128,2,3584]{2,1,0:T(2,128)(2,1)}, u32[]{:S(2)}, u32[]{:S(2)}) async-start(bf16[128,2,3584]{2,1,0:T(2,128)(2,1)} %reshape.190), calls=%async_computation | async-start | bytes 3670016 | tf_op jit(solution)/shard_map/all_to_all | solution.py:93
  46.8 0.4 iota_compare_fusion
  47.2 26.4 %all-to-all-done = bf16[128,2,3584]{2,1,0:T(2,128)(2,1)} async-done(((bf16[128,2,3584]{2,1,0:T(2,128)(2,1)}), bf16[128,2,3584]{2,1,0:T(2,128)(2,1)}, u32[]{:S(2)}, u32[]{:S(2)}) %all-to-all-start) | async-done | bytes 1835040 | tf_op jit(solution)/shard_map/all_to_all | solution.py:93
  73.6 4.1 %reshape.171 = bf16[256,3584]{1,0:T(8,128)(2,1)S(1)} reshape(bf16[128,2,3584]{2,1,0:T(2,128)(2,1)} %all-to-all-done) | data formatting | bytes 3670016 | tf_op jit(solution)/shard_map/reshape | solution.py:96
  77.6 2.0 gather_fusion.1
  79.7 1.8 multiply_reduce_fusion.1
  81.5 7.2 %convolution_convert_fusion = bf16[128,1792]{1,0:T(8,128)(2,1)S(1)} fusion(bf16[3584,1792]{1,0:T(8,128)(2,1)} %param.16, bf16[128,3584]{1,0:T(8,128)(2,1)} %param.11, bf16[128,3584]{1,0:T(8,128)(2,1)} %gather_fusion.1, f32[3584]{0:T(1024)S(1)} %copy-done.4, f32[128]{0:T(128)S(1)} %add_rsqrt_fusion), kind=kOutput, calls=%fused_computation.24 | convolution fusion | flops 1647149056 | bytes 15153664 | tf_op jit(solution)/shard_map/dot_general | solution.py:22
  88.7 0.3 copy.87
  89.0 16.7 %fusion = (f32[2,128,7]{1,2,0:T(8,128)S(1)}, f32[2,128,7,5120]{3,1,2,0:T(8,128)}) fusion(pred[128,5120]{1,0:T(8,128)(4,1)S(1)} %iota_compare_fusion, bf16[128,2,7,128]{0,3,2,1:T(8,128)(2,1)S(1)} %bitcast.95, bf16[1,2,2,5120,128]{4,3,2,1,0:T(8,128)(2,1)} %param.14), kind=kOutput, calls=%fused_computation.12 | convolution fusion | flops 2376333568 | bytes 40442880 | tf_op jit(solution)/shard_map/chgd,hld->hcgl/dot_general | solution.py:29
  105.8 1.5 scatter_custom_fusion.1
  107.3 4.6 %all-to-all-start.2 = ((f32[128,2,14]{2,1,0:T(2,128)}), f32[128,2,14]{2,1,0:T(2,128)S(1)}, u32[]{:S(2)}, u32[]{:S(2)}) async-start(f32[128,2,14]{2,1,0:T(2,128)} %bitcast.12), calls=%async_computation.2 | async-start | bytes 262144 | tf_op jit(solution)/shard_map/all_to_all | solution.py:127
  111.9 16.8 %exponential_reduce_fusion = f32[2,128,7]{1,2,0:T(8,128)S(1)} fusion(f32[2,128,7,5120]{3,1,2,0:T(8,128)} %get-tuple-element.21, f32[2,128,7]{1,2,0:T(8,128)S(1)} %get-tuple-element.20, pred[128,5120]{1,0:T(8,128)(4,1)S(1)} %iota_compare_fusion), kind=kLoop, calls=%fused_computation.10 | loop fusion | flops 36698368 | bytes 37369856 | tf_op jit(solution)/shard_map/reduce_sum | solution.py:106
  128.9 1.5 scatter_custom_fusion.2
  130.4 10.0 %all-to-all-start.3 = ((f32[128,2,14]{2,1,0:T(2,128)}), f32[128,2,14]{2,1,0:T(2,128)S(1)}, u32[]{:S(2)}, u32[]{:S(2)}) async-start(f32[128,2,14]{2,1,0:T(2,128)} %bitcast.15), calls=%async_computation.3 | async-start | bytes 262144 | tf_op jit(solution)/shard_map/all_to_all | solution.py:134
  140.3 1.6 scatter_custom_fusion
  141.9 1.3 reshape.188
  143.2 6.3 %all-to-all-done.3 = f32[128,2,14]{2,1,0:T(2,128)S(1)} async-done(((f32[128,2,14]{2,1,0:T(2,128)}), f32[128,2,14]{2,1,0:T(2,128)S(1)}, u32[]{:S(2)}, u32[]{:S(2)}) %all-to-all-start.3) | async-done | bytes 14368 | tf_op jit(solution)/shard_map/all_to_all | solution.py:134
  149.5 4.8 %all-to-all-start.1 = ((bf16[128,2,1792]{2,1,0:T(2,128)(2,1)}), bf16[128,2,1792]{2,1,0:T(2,128)(2,1)S(1)}, u32[]{:S(2)}, u32[]{:S(2)}) async-start(bf16[128,2,1792]{2,1,0:T(2,128)(2,1)} %reshape.188), calls=%async_computation.1 | async-start | bytes 1835008 | tf_op jit(solution)/shard_map/all_to_all | solution.py:120
  154.7 15.8 %gather_fusion.2 = bf16[256,2,2,128,128]{4,3,2,1,0:T(8,128)(2,1)} fusion(bf16[32,2,2,128,128]{4,3,2,1,0:T(8,128)(2,1)} %param.13, s32[1024]{0:T(1024)S(1)} %pad_clamp_fusion), kind=kCustom, calls=%fused_computation.2 | custom fusion | bytes 67109888 | tf_op jit(solution)/shard_map/gather | solution.py:142
  170.4 0.2 reshape.177
  170.8 0.3 reshape.180
  171.2 0.9 all-to-all-done.1
  172.1 1.6 reshape.173
  173.7 13.6 %multiply_reduce_fusion = (f32[2,256,7]{2,1,0:T(8,128)S(1)}, f32[2,256,7,128]{3,2,1,0:T(8,128)}) fusion(bf16[256,2,7,128]{3,2,1,0:T(8,128)(2,1)} %reshape.173, bf16[256,2,2,128,128]{4,3,2,1,0:T(8,128)(2,1)} %gather_fusion.2), kind=kOutput, calls=%fused_computation.27 | convolution fusion | flops 118354432 | bytes 19675136 | tf_op jit(solution)/shard_map/chgd,chtd->hcgt/dot_general | solution.py:145
  187.5 2.5 fusion.9
  190.2 9.8 %fusion.2 = f32[256,2,7,128]{3,2,1,0:T(8,128)} fusion(bf16[256,2,2,128,128]{4,3,2,1,0:T(8,128)(2,1)} %gather_fusion.2, f32[2,256,7,128]{3,2,1,0:T(8,128)} %get-tuple-element.19, f32[2,256,7]{2,1,0:T(8,128)S(1)} %fusion.23, f32[2,256,7]{2,1,0:T(8,128)S(1)} %bitcast_maximum_fusion), kind=kOutput, calls=%fused_computation.15 | convolution fusion | flops 119275520 | bytes 20738048 | tf_op jit(solution)/shard_map/hcgt,chtd->chgd/dot_general | solution.py:158
  199.9 2.3 reshape.181
  202.3 0.2 copy.104
  202.5 0.3 reshape_reshape.7
  202.7 0.2 copy.100
  202.9 0.3 reshape_reshape.6
  203.2 4.2 %concatenate.3 = f32[128,2,1820]{2,1,0:T(2,128)} concatenate(f32[128,2,1792]{2,1,0:T(2,128)S(1)} %reshape.181, f32[128,2,14]{2,1,0:T(2,128)S(1)} %reshape_reshape.6, f32[128,2,14]{2,1,0:T(2,128)S(1)} %reshape_reshape.7), dimensions={2} | concatenate | bytes 3727360 | tf_op jit(solution)/shard_map/concatenate | solution.py:13
  207.4 9.4 %all-to-all-start.4 = ((f32[128,2,1820]{2,1,0:T(2,128)}), f32[128,2,1820]{2,1,0:T(2,128)}, u32[]{:S(2)}, u32[]{:S(2)}) async-start(f32[128,2,1820]{2,1,0:T(2,128)} %concatenate.3), calls=%async_computation.4 | async-start | bytes 3932160 | tf_op jit(solution)/shard_map/all_to_all | solution.py:14
  216.8 3.4 %convolution_convert_fusion.1 = bf16[128,512]{1,0:T(8,128)(2,1)} fusion(bf16[3584,512]{1,0:T(8,128)(2,1)} %param.17, bf16[128,3584]{1,0:T(8,128)(2,1)S(1)} %copy-done.3, bf16[128,3584]{1,0:T(8,128)(2,1)S(1)} %copy-done.2, f32[3584]{0:T(1024)S(1)} %copy-done.4, f32[128]{0:T(128)S(1)} %add_rsqrt_fusion), kind=kOutput, calls=%fused_computation.35 | convolution fusion | flops 472580096 | bytes 5650944 | tf_op jit(solution)/shard_map/dot_general | solution.py:23
  220.2 25.2 %all-to-all-done.4 = f32[128,2,1820]{2,1,0:T(2,128)} async-done(((f32[128,2,1820]{2,1,0:T(2,128)}), f32[128,2,1820]{2,1,0:T(2,128)}, u32[]{:S(2)}, u32[]{:S(2)}) %all-to-all-start.4) | async-done | bytes 1863712 | tf_op jit(solution)/shard_map/all_to_all | solution.py:14
  245.4 2.9 %split.14 = f32[128,2,1792]{2,1,0:T(2,128)} slice(f32[128,2,1820]{2,1,0:T(2,128)} %all-to-all-done.4), slice={[0:128], [0:2], [0:1792]} | slice | bytes 3670016 | tf_op jit(solution)/shard_map/split | solution.py:15
  248.2 2.5 reshape.186
  250.8 1.9 gather_fusion.5
  252.7 1.5 copy.108
  254.2 1.2 fusion.40
  255.3 0.6 gather_fusion.3
  256.1 0.7 gather_fusion.4
  256.8 18.4 %fusion.16 = bf16[128,2,7,128]{0,3,2,1:T(8,128)(2,1)S(1)} fusion(f32[128,2,7,128]{0,3,2,1:T(8,128)S(1)} %bitcast.98, bf16[1,2,2,5120,128]{4,3,2,1,0:T(8,128)(2,1)} %param.14, f32[2,128,7,5120]{3,1,2,0:T(8,128)} %get-tuple-element.21, f32[2,128,7]{1,2,0:T(8,128)S(1)} %bitcast.105, f32[2,128,7]{1,2,0:T(8,128)S(1)} %bitcast.104, ...), kind=kOutput, calls=%fused_computation.34 | convolution fusion | flops 2395144192 | bytes 41367552 | tf_op jit(solution)/shard_map/hcgl,hld->chgd/dot_general | solution.py:176
  275.2 1.0 copy.109
  (50 shorter events, 2.1 us)
Async XLA Ops:
  0.6 34.2 %copy-start = (bf16[32,3584]{1,0:T(8,128)(2,1)S(1)}, bf16[32,3584]{1,0:T(8,128)(2,1)}, u32[]{:S(2)}) copy-start(bf16[32,3584]{1,0:T(8,128)(2,1)} %param.12) | copy-start | bytes 688132
  38.2 8.3 %copy-start.5 = (s32[128]{0:T(128)S(1)}, s32[128]{0:T(128)}, u32[]{:S(2)}) copy-start(s32[128]{0:T(128)} %param.9) | copy-start | bytes 1540
  38.2 8.5 %copy-start.6 = (s32[128]{0:T(128)S(1)}, s32[128]{0:T(128)}, u32[]{:S(2)}) copy-start(s32[128]{0:T(128)} %param.10) | copy-start | bytes 1540
  38.2 35.3 %all-to-all-start = ((bf16[128,2,3584]{2,1,0:T(2,128)(2,1)}), bf16[128,2,3584]{2,1,0:T(2,128)(2,1)}, u32[]{:S(2)}, u32[]{:S(2)}) async-start(bf16[128,2,3584]{2,1,0:T(2,128)(2,1)} %reshape.190), calls=%async_computation | async-start | bytes 3670016 | tf_op jit(solution)/shard_map/all_to_all | solution.py:93
  77.6 3.9 %copy-start.4 = (f32[3584]{0:T(1024)S(1)}, f32[3584]{0:T(1024)}, u32[]{:S(2)}) copy-start(f32[3584]{0:T(1024)} %param.15) | copy-start | bytes 43012
  107.3 23.1 %all-to-all-start.2 = ((f32[128,2,14]{2,1,0:T(2,128)}), f32[128,2,14]{2,1,0:T(2,128)S(1)}, u32[]{:S(2)}, u32[]{:S(2)}) async-start(f32[128,2,14]{2,1,0:T(2,128)} %bitcast.12), calls=%async_computation.2 | async-start | bytes 262144 | tf_op jit(solution)/shard_map/all_to_all | solution.py:127
  130.4 19.2 %all-to-all-start.3 = ((f32[128,2,14]{2,1,0:T(2,128)}), f32[128,2,14]{2,1,0:T(2,128)S(1)}, u32[]{:S(2)}, u32[]{:S(2)}) async-start(f32[128,2,14]{2,1,0:T(2,128)} %bitcast.15), calls=%async_computation.3 | async-start | bytes 262144 | tf_op jit(solution)/shard_map/all_to_all | solution.py:134
  149.5 22.6 %all-to-all-start.1 = ((bf16[128,2,1792]{2,1,0:T(2,128)(2,1)}), bf16[128,2,1792]{2,1,0:T(2,128)(2,1)S(1)}, u32[]{:S(2)}, u32[]{:S(2)}) async-start(bf16[128,2,1792]{2,1,0:T(2,128)(2,1)} %reshape.188), calls=%async_computation.1 | async-start | bytes 1835008 | tf_op jit(solution)/shard_map/all_to_all | solution.py:120
  207.4 9.4 %copy-start.2 = (bf16[128,3584]{1,0:T(8,128)(2,1)S(1)}, bf16[128,3584]{1,0:T(8,128)(2,1)}, u32[]{:S(2)}) copy-start(bf16[128,3584]{1,0:T(8,128)(2,1)} %gather_fusion.1) | copy-start | bytes 2752516
  207.4 9.4 %copy-start.3 = (bf16[128,3584]{1,0:T(8,128)(2,1)S(1)}, bf16[128,3584]{1,0:T(8,128)(2,1)}, u32[]{:S(2)}) copy-start(bf16[128,3584]{1,0:T(8,128)(2,1)} %param.11) | copy-start | bytes 2752516
  207.4 38.0 %all-to-all-start.4 = ((f32[128,2,1820]{2,1,0:T(2,128)}), f32[128,2,1820]{2,1,0:T(2,128)}, u32[]{:S(2)}, u32[]{:S(2)}) async-start(f32[128,2,1820]{2,1,0:T(2,128)} %concatenate.3), calls=%async_computation.4 | async-start | bytes 3932160 | tf_op jit(solution)/shard_map/all_to_all | solution.py:14
  256.8 19.4 %copy-start.1 = (bf16[32,3584]{1,0:T(8,128)(2,1)S(1)}, bf16[32,3584]{1,0:T(8,128)(2,1)}, u32[]{:S(2)}) copy-start(bf16[32,3584]{1,0:T(8,128)(2,1)} %param.12) | copy-start | bytes 688132
where the time goes:
time: 278 us; the launch traced here: 276 us
  matrix products  69 us (25%)
  waiting for transfers between devices  58.8 us (21%)
  local copies, waits for them, and re-layouts  54.6 us (20%)
  starting transfers between devices  37.1 us (13%)
  blocking collectives  33.3 us (12%)
  other arithmetic  22.3 us (8%)
    all_gather x1, blocking collectives, local(): whole_map = lax.all_gather(child_parent, ('row', 'col'), axis=0, tiled=True)  33.3 us
    all_to_all x1, waiting for transfers between devices, local(): lax.all_to_all(parent_hidden[send_ids], ('row', 'col'), split_axis=0, con...  26.4 us
    all_to_all x1, waiting for transfers between devices, side_by_side(): lax.all_to_all(both, axis, split_axis=split_dim, concat_axis=concat_dim,...  25.2 us
    dot_general x1, matrix products, local(): jnp.einsum('hcgl,hld->chgd', weight_pre, prefix_rows[1], preferred_elemen...  18.4 us
    reduce_sum x1, other arithmetic, local(): sum_pre = jnp.sum(jnp.exp(score_pre - top_pre), axis=-1, keepdims=True)  16.8 us
    dot_general x1, matrix products, prefix_scores(): jnp.einsum('chgd,hld->hcgl', grouped, prefix_rows[0], preferred_element_t...  16.7 us
    gather x1, local copies, waits for them, and re-layouts, local(): own_blocks = parent_cache[send_ids.reshape(-1)]  15.8 us
    dot_general x1, matrix products, local(): jnp.einsum('chgd,chtd->hcgt', item_query, own_blocks[:, 0], preferred_ele...  13.6 us
  transfers between devices with their start and end apart: 5, of which 4 were waited for; matrix products, arithmetic and copies ran while one was open for 15% of the time, Pallas kernels for 0%

commit v1 on v0

v1 whole, which is shorter than its diff:
```python
import functools
import math

import jax
import jax.numpy as jnp
from jax import lax
from jax.experimental import pallas as pl
from jax.experimental.pallas import tpu as pltpu
from jax.sharding import PartitionSpec as P

EPSILON = 1e-06
F32 = jnp.float32
BF16 = jnp.bfloat16
I32 = jnp.int32
ROWS = 16
COLS = 8
N = 128
D = 3584
HEADS = 14
GROUP = 7
DH = 128
PARENTS = 32
BLOCK = 128
DELTA_CHUNKS = 2
CHUNK = D // DELTA_CHUNKS
HALF = CHUNK // 2
BACK_CHUNKS = 3
SHARE_CHUNKS = 2
TILE = 32
KEYS = 512
SCORE_SCALE = math.log2(math.e) / math.sqrt(DH)


def iotas(shape):
    return lax.broadcasted_iota(I32, shape, 0), lax.broadcasted_iota(I32, shape, 1)


def one_zero(mask, kind=BF16):
    return jnp.where(mask, 1.0, 0.0).astype(kind)


def to_col(row):
    below, along = iotas((N, N))
    return jnp.sum(jnp.where(below == along, row, 0.0), axis=1, keepdims=True)


def to_row(col):
    below, along = iotas((N, N))
    return jnp.sum(jnp.where(below == along, col, 0.0), axis=0, keepdims=True)


def rank_row(key_row, key_col):
    below, along = iotas((N, N))
    earlier = (key_col == key_row) & (below < along)
    return jnp.sum(jnp.where(earlier, 1.0, 0.0), axis=0, keepdims=True)


def column_order(ids):
    column = ((ids >> 5) & (COLS - 1)).astype(F32)
    return column * 16.0 + rank_row(column, to_col(column))


def dot(a, b):
    return jnp.dot(a, b, preferred_element_type=F32)


def dot_t(a, b):
    return lax.dot_general(a, b, (((1,), (1,)), ((), ())), preferred_element_type=F32)


def pair_rows(left, right):
    width = left.shape[1]
    both = jnp.concatenate(
        [left.reshape(ROWS, 1, 8, width), right.reshape(ROWS, 1, 8, width)], axis=1
    )
    return both.reshape(2 * N, width)


class Exchange:
    def __init__(self, axis, count, me, rows):
        self.axis, self.count, self.me, self.rows = axis, count, me, rows

    def part(self, ref, k):
        return ref.at[pl.ds(pl.multiple_of(k * self.rows, self.rows), self.rows)]

    def copy(self, src, dst, send, recv, k, slot):
        return pltpu.make_async_remote_copy(
            src_ref=self.part(src, k),
            dst_ref=self.part(dst, slot),
            send_sem=send.at[k],
            recv_sem=recv.at[slot],
            device_id={self.axis: k},
            device_id_type=pl.DeviceIdType.MESH,
        )

    def each(self, act):
        def body(k, carry):
            act(lax.rem(self.me + k, self.count))
            return carry

        lax.fori_loop(1, self.count, body, 0)

    def start(self, src, dst, send, recv):
        self.each(lambda k: self.copy(src, dst, send, recv, k, self.me).start())
        own = pl.ds(pl.multiple_of(self.me * self.rows, self.rows), self.rows)
        dst[own, :] = src[own, :]

    def arrived(self, src, dst, send, recv):
        self.each(lambda k: self.copy(src, dst, send, recv, k, k).wait_recv())

    def sent(self, src, dst, send, recv):
        self.each(lambda k: self.copy(src, dst, send, recv, k, self.me).wait_send())


def parent_kernel(
    ids_ref,
    gain_ref,
    delta_hbm,
    hidden_hbm,
    blocks_hbm,
    wq_hbm,
    wkv_hbm,
    back_ref,
    share_ref,
    delta_v,
    hidden_v,
    blocks_v,
    weight_v,
    out1,
    in1,
    out2,
    in2,
    id_out1,
    id_in1,
    id_out2,
    id_in2,
    wide,
    normed,
    heads_v,
    back1,
    back1_in,
    back2,
    score,
    total,
    prob,
    stat,
    share1,
    share1_in,
    share2,
    load_sem,
    d1s,
    d1r,
    d2s,
    d2r,
    i1s,
    i1r,
    i2s,
    i2r,
    b1s,
    b1r,
    b2s,
    b2r,
    s1s,
    s1r,
    s2s,
    s2r,
):
    my_row = lax.axis_index("row")
    my_col = lax.axis_index("col")
    load_delta = pltpu.make_async_copy(delta_hbm, delta_v, load_sem.at[0])
    load_delta.start()

    barrier = pltpu.get_barrier_semaphore()

    def greet_col(k, carry):
        pl.semaphore_signal(
            barrier,
            inc=1,
            device_id={"col": lax.rem(my_col + k, COLS)},
            device_id_type=pl.DeviceIdType.MESH,
        )
        return carry

    def greet_row(k, carry):
        pl.semaphore_signal(
            barrier,
            inc=1,
            device_id={"row": lax.rem(my_row + k, ROWS)},
            device_id_type=pl.DeviceIdType.MESH,
        )
        return carry

    lax.fori_loop(1, COLS, greet_col, 0)
    lax.fori_loop(1, ROWS, greet_row, 0)

    below, along = iotas((N, N))
    ids = ids_ref[...]
    order = column_order(ids)
    pick = order == below.astype(F32)
    sorting = one_zero(pick)
    far_row = (ids >> 8).astype(F32)
    far_local = (ids & (PARENTS - 1)).astype(F32)
    row_sorted = jnp.sum(jnp.where(pick, far_row, 0.0), axis=1, keepdims=True)
    local_sorted = jnp.sum(jnp.where(pick, far_local, 0.0), axis=1, keepdims=True)
    id_out1[...] = jnp.where(along < 64, row_sorted, local_sorted).astype(BF16)

    load_delta.wait()
    loads = [
        pltpu.make_async_copy(hidden_hbm, hidden_v, load_sem.at[1]),
        pltpu.make_async_copy(wq_hbm, weight_v.at[:, pl.ds(0, HEADS * DH)], load_sem.at[2]),
        pltpu.make_async_copy(wkv_hbm, weight_v.at[:, pl.ds(HEADS * DH, 512)], load_sem.at[3]),
        pltpu.make_async_copy(blocks_hbm, blocks_v, load_sem.at[4]),
    ]

    by_col = Exchange("col", COLS, my_col, 16)
    by_row = Exchange("row", ROWS, my_row, 16)
    by_row8 = Exchange("row", ROWS, my_row, 8)

    pl.semaphore_wait(barrier, COLS + ROWS - 2)
    by_col.start(id_out1, id_in1, i1s, i1r)
    for c in range(DELTA_CHUNKS):
        out1[c] = dot(sorting, delta_v[:, c * CHUNK : (c + 1) * CHUNK]).astype(BF16)
        by_col.start(out1.at[c], in1.at[c], d1s.at[c], d1r.at[c])
    for load in loads:
        load.start()

    by_col.arrived(id_out1, id_in1, i1s, i1r)
    arrived_ids = id_in1[...].astype(F32)
    row_col = arrived_ids[:, 0:1]
    row_row = to_row(row_col)
    local_row = to_row(arrived_ids[:, 64:65])
    place = row_row * 8.0 + rank_row(row_row, row_col)
    place_col = to_col(place)
    place_pick = place == below.astype(F32)
    id_out2[...] = jnp.broadcast_to(
        jnp.sum(jnp.where(place_pick, local_row, 0.0), axis=1, keepdims=True), (N, N)
    )
    by_row8.start(id_out2, id_in2, i2s, i2r)

    wide_below, wide_along = iotas((2 * N, 2 * N))
    code_below = ((wide_below >> 4) * 16 + (wide_below & 7) * 2 + ((wide_below >> 3) & 1)).astype(
        F32
    )
    code_along = ((wide_along >> 4) * 16 + (wide_along & 7) * 2 + ((wide_along >> 3) & 1)).astype(
        F32
    )
    code_row = jnp.concatenate([place * 2.0, place * 2.0 + 1.0], axis=1)
    code_col = jnp.concatenate([place_col * 2.0, place_col * 2.0 + 1.0], axis=0)
    forth = one_zero(code_below == code_row)
    turn = one_zero(code_along == code_col)

    for c in range(DELTA_CHUNKS):
        by_col.arrived(out1.at[c], in1.at[c], d1s.at[c], d1r.at[c])
        stacked = jnp.concatenate([in1[c, :, :HALF], in1[c, :, HALF:]], axis=0)
        out2[c] = dot(forth, stacked).astype(BF16)
        by_row.start(out2.at[c], in2.at[c], d2s.at[c], d2r.at[c])

    loads[0].wait()
    by_row8.arrived(id_out2, id_in2, i2s, i2r)
    local_id = id_in2[...]
    owner = one_zero(local_id[:, :PARENTS] == along[:, :PARENTS].astype(F32))
    squares = jnp.zeros((N, 1), F32)
    for c in range(DELTA_CHUNKS):
        by_row.arrived(out2.at[c], in2.at[c], d2s.at[c], d2r.at[c])
        for half in range(2):
            for w in range(HALF // 128):
                at = c * CHUNK + half * HALF + w * 128
                grid = in2[c, :, w * 128 : (w + 1) * 128].astype(F32)
                grid = grid.reshape(ROWS, 2, 8, 128)[:, half].reshape(N, 128)
                value = dot(owner, hidden_v[:, at : at + 128]) + grid
                wide[:, at : at + 128] = value
                squares = squares + jnp.sum(value * value, axis=1, keepdims=True)
    inverse = lax.rsqrt(squares / D + EPSILON)
    for w in range(D // 128):
        at = w * 128
        normed[:, at : at + 128] = (
            wide[:, at : at + 128] * inverse * gain_ref[:, at : at + 128]
        ).astype(BF16)

    loads[1].wait()
    loads[2].wait()
    for c in range(BACK_CHUNKS):

        def project(t, carry, c=c):
            n = c * 3 + t
            y = dot(normed[...], weight_v[:, pl.ds(pl.multiple_of(n * 256, 256), 256)])
            heads_v[2 * n] = y[:, :128].astype(BF16)
            heads_v[2 * n + 1] = y[:, 128:].astype(BF16)
            back1[c, :, pl.ds(pl.multiple_of(t * 128, 128), 128)] = pair_rows(
                y[:, :128], y[:, 128:]
            ).astype(BF16)
            return carry

        lax.fori_loop(0, 3, project, 0)
        by_row.start(back1.at[c], back1_in.at[c], b1s.at[c], b1r.at[c])

    loads[3].wait()
    score[...] = jnp.zeros_like(score)
    total[...] = jnp.zeros_like(total)

    def masks(k):
        first = (2 * k).astype(F32)
        return one_zero(local_id == first), one_zero(local_id == first + 1.0)

    def score_pair(k, carry):
        mask0, mask1 = masks(k)
        for g in range(2):
            keys = jnp.concatenate([blocks_v[2 * k, 0, g], blocks_v[2 * k + 1, 0, g]], axis=1)
            for h in range(g * GROUP, (g + 1) * GROUP):
                q = heads_v[h]
                score[h] += dot_t(jnp.concatenate([q * mask0, q * mask1], axis=1), keys)
        return carry

    lax.fori_loop(0, PARENTS // 2, score_pair, 0)

    for c in range(BACK_CHUNKS):
        by_row.arrived(back1.at[c], back1_in.at[c], b1s.at[c], b1r.at[c])
        turned = dot(turn, back1_in[c]).astype(BF16)
        for t in range(3):
            back2[c, :, t * 256 : t * 256 + 128] = turned[:N, t * 128 : (t + 1) * 128]
            back2[c, :, t * 256 + 128 : (t + 1) * 256] = turned[N:, t * 128 : (t + 1) * 128]
        by_col.start(back2.at[c], back_ref.at[c], b2s.at[c], b2r.at[c])

    for g in range(2):
        stats = jnp.zeros((N, N), F32)
        for h in range(GROUP):
            s = score[g * GROUP + h] * SCORE_SCALE
            top = jnp.max(s, axis=1, keepdims=True)
            e = jnp.exp2(s - top)
            prob[g * GROUP + h] = e.astype(BF16)
            stats = jnp.where(along == h, top, stats)
            stats = jnp.where(along == 8 + h, jnp.sum(e, axis=1, keepdims=True), stats)
        stat[g] = stats

    def value_pair(k, carry):
        mask0, mask1 = masks(k)
        for g in range(2):
            values = jnp.concatenate([blocks_v[2 * k, 1, g], blocks_v[2 * k + 1, 1, g]], axis=0)
            for h in range(g * GROUP, (g + 1) * GROUP):
                p = prob[h]
                total[h] += dot(jnp.concatenate([p * mask0, p * mask1], axis=1), values)
        return carry

    lax.fori_loop(0, PARENTS // 2, value_pair, 0)

    for c in range(SHARE_CHUNKS):
        for b in range(4):
            h = c * 4 + b
            sides = []
            for g in range(2):
                stats = stat[g]
                if h < GROUP:
                    sides.append(total[g * GROUP + h] / stats[:, 8 + h : 9 + h])
                else:
                    high = stats.astype(BF16).astype(F32)
                    rest = stats - high
                    middle = rest.astype(BF16).astype(F32)
                    low = rest - middle
                    sides.append(
                        high + pltpu.roll(middle, shift=16, axis=1) + pltpu.roll(low, shift=32, axis=1)
                    )
            share1[c, :, b * 128 : (b + 1) * 128] = pair_rows(sides[0], sides[1]).astype(BF16)
        by_row.start(share1.at[c], share1_in.at[c], s1s.at[c], s1r.at[c])

    for c in range(SHARE_CHUNKS):
        by_row.arrived(share1.at[c], share1_in.at[c], s1s.at[c], s1r.at[c])
        turned = dot(turn, share1_in[c]).astype(BF16)
        share2[c, :, :512] = turned[:N]
        share2[c, :, 512:] = turned[N:]
        by_col.start(share2.at[c], share_ref.at[c], s2s.at[c], s2r.at[c])

    for c in range(BACK_CHUNKS):
        by_col.arrived(back2.at[c], back_ref.at[c], b2s.at[c], b2r.at[c])
    for c in range(SHARE_CHUNKS):
        by_col.arrived(share2.at[c], share_ref.at[c], s2s.at[c], s2r.at[c])

    by_col.sent(id_out1, id_in1, i1s, i1r)
    by_row8.sent(id_out2, id_in2, i2s, i2r)
    for c in range(DELTA_CHUNKS):
        by_col.sent(out1.at[c], in1.at[c], d1s.at[c], d1r.at[c])
        by_row.sent(out2.at[c], in2.at[c], d2s.at[c], d2r.at[c])
    for c in range(BACK_CHUNKS):
        by_row.sent(back1.at[c], back1_in.at[c], b1s.at[c], b1r.at[c])
        by_col.sent(back2.at[c], back_ref.at[c], b2s.at[c], b2r.at[c])
    for c in range(SHARE_CHUNKS):
        by_row.sent(share1.at[c], share1_in.at[c], s1s.at[c], s1r.at[c])
        by_col.sent(share2.at[c], share_ref.at[c], s2s.at[c], s2r.at[c])


def prefix_kernel(
    ids_ref,
    lens_ref,
    back_ref,
    share_ref,
    prefix_hbm,
    context_ref,
    kv_ref,
    keys_v,
    values_v,
    query_v,
    part_v,
    stat_v,
    result_v,
    top,
    mass,
    total,
    load_sem,
):
    loads = []
    for g in range(2):
        loads.append(
            pltpu.make_async_copy(prefix_hbm.at[0, g], keys_v.at[g], load_sem.at[2 * g])
        )
        loads.append(
            pltpu.make_async_copy(prefix_hbm.at[1, g], values_v.at[g], load_sem.at[2 * g + 1])
        )
    for load in loads:
        load.start()

    below, along = iotas((N, N))
    along_f = along.astype(F32)
    below_f = below.astype(F32)
    arrive_col = to_col(column_order(ids_ref[...]))
    lens = lens_ref[...].astype(F32)
    lens_col = to_col(lens)
    before = (lens_col > lens) | ((lens_col == lens) & (below < along))
    place = jnp.sum(jnp.where(before, 1.0, 0.0), axis=0, keepdims=True)
    place_col = to_col(place)
    unsort1 = one_zero(arrive_col == along_f)
    pick = place == below_f
    gather = dot(one_zero(pick), unsort1).astype(BF16)
    sorted_lens = jnp.sum(jnp.where(pick, lens, 0.0), axis=1, keepdims=True)

    for n in range(GROUP):
        c, t = n // 3, n % 3
        query_v[:, n * 256 : (n + 1) * 256] = dot(
            gather, back_ref[c, :, t * 256 : (t + 1) * 256]
        ).astype(BF16)
    for n in range(2):
        kv_ref[:, n * 256 : (n + 1) * 256] = dot(
            unsort1, back_ref[2, :, (n + 1) * 256 : (n + 2) * 256]
        ).astype(BF16)
    for g in range(2):
        for h in range(GROUP):
            c, b = h // 4, h % 4
            part_v[:, (g * GROUP + h) * 128 : (g * GROUP + h + 1) * 128] = dot(
                gather, share_ref[c, :, g * 512 + b * 128 : g * 512 + (b + 1) * 128]
            )
        packed = dot(gather, share_ref[1, :, g * 512 + 384 : g * 512 + 512])
        stat_v[g] = (
            packed
            + pltpu.roll(packed, shift=N - 16, axis=1)
            + pltpu.roll(packed, shift=N - 32, axis=1)
        )

    for g in range(2):
        loads[2 * g].wait()
        loads[2 * g + 1].wait()
        for t in range(N // TILE):
            rows = slice(t * TILE, (t + 1) * TILE)
            limit = jnp.concatenate([sorted_lens[rows] * float(BLOCK)] * GROUP, axis=0)
            longest = jnp.max(sorted_lens[rows]).astype(I32)
            steps = (longest * BLOCK + KEYS - 1) // KEYS
            q = jnp.concatenate(
                [
                    query_v[rows, (g * GROUP + h) * 128 : (g * GROUP + h + 1) * 128]
                    for h in range(GROUP)
                ],
                axis=0,
            )
            top[...] = jnp.full_like(top, -jnp.inf)
            mass[...] = jnp.zeros_like(mass)
            total[...] = jnp.zeros_like(total)

            def step(j, carry, g=g, q=q, limit=limit):
                start = pl.multiple_of(j * KEYS, KEYS)
                s = dot_t(q, keys_v[g, pl.ds(start, KEYS), :]) * SCORE_SCALE
                spot = lax.broadcasted_iota(I32, s.shape, 1).astype(F32) + start.astype(F32)
                s = jnp.where(spot < limit, s, -jnp.inf)
                old = top[...]
                new = jnp.maximum(old, jnp.max(s, axis=1, keepdims=True))
                p = jnp.exp2(s - new)
                shrink = jnp.exp2(old - new)
                mass[...] = mass[...] * shrink + jnp.sum(p, axis=1, keepdims=True)
                total[...] = total[...] * shrink + dot(
                    p.astype(BF16), values_v[g, pl.ds(start, KEYS), :]
                )
                top[...] = new
                return carry

            lax.fori_loop(0, steps, step, 0)
            stats = stat_v[g, rows]
            for h in range(GROUP):
                at = (g * GROUP + h) * 128
                own = slice(h * TILE, (h + 1) * TILE)
                top_par = stats[:, h : h + 1]
                mass_par = stats[:, 8 + h : 9 + h]
                top_all = jnp.maximum(top[own], top_par)
                near = jnp.exp2(top[own] - top_all)
                far = jnp.exp2(top_par - top_all) * mass_par
                whole = mass[own] * near + far
                result_v[rows, at : at + 128] = (
                    (total[own] * near + part_v[rows, at : at + 128] * far) / whole
                ).astype(BF16)

    unsort = one_zero(place_col == along_f)
    for n in range(GROUP):
        context_ref[:, n * 256 : (n + 1) * 256] = dot(
            unsort, result_v[:, n * 256 : (n + 1) * 256]
        ).astype(BF16)


def local(
    child_parent,
    prefix_len,
    child_delta,
    parent_hidden,
    parent_cache,
    prefix_cache,
    norm_gain,
    w_query,
    w_kv,
):
    vmem = pl.BlockSpec(memory_space=pltpu.VMEM)
    hbm = pl.BlockSpec(memory_space=pl.ANY)
    dma = pltpu.SemaphoreType.DMA
    ids = child_parent.reshape(1, N)
    lens = prefix_len.reshape(1, N)
    back_shape = (BACK_CHUNKS, N, 768)
    share_shape = (SHARE_CHUNKS, N, 1024)
    back, share = pl.pallas_call(
        parent_kernel,
        name="parent_side",
        out_shape=(
            jax.ShapeDtypeStruct(back_shape, BF16),
            jax.ShapeDtypeStruct(share_shape, BF16),
        ),
        in_specs=[vmem, vmem, hbm, hbm, hbm, hbm, hbm],
        out_specs=(vmem, vmem),
        scratch_shapes=[
            pltpu.VMEM((N, D), BF16),
            pltpu.VMEM((PARENTS, D), BF16),
            pltpu.VMEM((PARENTS, 2, 2, BLOCK, DH), BF16),
            pltpu.VMEM((D, 2304), BF16),
            pltpu.VMEM((DELTA_CHUNKS, N, CHUNK), BF16),
            pltpu.VMEM((DELTA_CHUNKS, N, CHUNK), BF16),
            pltpu.VMEM((DELTA_CHUNKS, 2 * N, HALF), BF16),
            pltpu.VMEM((DELTA_CHUNKS, 2 * N, HALF), BF16),
            pltpu.VMEM((N, N), BF16),
            pltpu.VMEM((N, N), BF16),
            pltpu.VMEM((N, N), F32),
            pltpu.VMEM((N, N), F32),
            pltpu.VMEM((N, D), F32),
            pltpu.VMEM((N, D), BF16),
            pltpu.VMEM((18, N, 128), BF16),
            pltpu.VMEM((BACK_CHUNKS, 2 * N, 384), BF16),
            pltpu.VMEM((BACK_CHUNKS, 2 * N, 384), BF16),
            pltpu.VMEM(back_shape, BF16),
            pltpu.VMEM((HEADS, N, BLOCK), F32),
            pltpu.VMEM((HEADS, N, DH), F32),
            pltpu.VMEM((HEADS, N, BLOCK), BF16),
            pltpu.VMEM((2, N, N), F32),
            pltpu.VMEM((SHARE_CHUNKS, 2 * N, 512), BF16),
            pltpu.VMEM((SHARE_CHUNKS, 2 * N, 512), BF16),
            pltpu.VMEM(share_shape, BF16),
            dma((5,)),
            dma((DELTA_CHUNKS, COLS)),
            dma((DELTA_CHUNKS, COLS)),
            dma((DELTA_CHUNKS, ROWS)),
            dma((DELTA_CHUNKS, ROWS)),
            dma((COLS,)),
            dma((COLS,)),
            dma((ROWS,)),
            dma((ROWS,)),
            dma((BACK_CHUNKS, ROWS)),
            dma((BACK_CHUNKS, ROWS)),
            dma((BACK_CHUNKS, COLS)),
            dma((BACK_CHUNKS, COLS)),
            dma((SHARE_CHUNKS, ROWS)),
            dma((SHARE_CHUNKS, ROWS)),
            dma((SHARE_CHUNKS, COLS)),
            dma((SHARE_CHUNKS, COLS)),
        ],
        compiler_params=pltpu.CompilerParams(
            collective_id=0, has_side_effects=True, vmem_limit_bytes=56 << 20
        ),
    )(ids, norm_gain.reshape(1, D), child_delta, parent_hidden, parent_cache, w_query, w_kv)
    tokens = prefix_cache.shape[3]
    context, new_kv = pl.pallas_call(
        prefix_kernel,
        name="prefix_side",
        out_shape=(
            jax.ShapeDtypeStruct((N, HEADS * DH), BF16),
            jax.ShapeDtypeStruct((N, 512), BF16),
        ),
        in_specs=[vmem, vmem, vmem, vmem, hbm],
        out_specs=(vmem, vmem),
        scratch_shapes=[
            pltpu.VMEM((2, tokens, DH), BF16),
            pltpu.VMEM((2, tokens, DH), BF16),
            pltpu.VMEM((N, HEADS * DH), BF16),
            pltpu.VMEM((N, HEADS * DH), F32),
            pltpu.VMEM((2, N, N), F32),
            pltpu.VMEM((N, HEADS * DH), BF16),
            pltpu.VMEM((GROUP * TILE, 1), F32),
            pltpu.VMEM((GROUP * TILE, 1), F32),
            pltpu.VMEM((GROUP * TILE, DH), F32),
            dma((4,)),
        ],
        compiler_params=pltpu.CompilerParams(vmem_limit_bytes=40 << 20),
    )(ids, lens, back, share, prefix_cache.reshape(prefix_cache.shape[1:]))
    return context, new_kv


def solution(mesh):
    return jax.shard_map(
        local,
        mesh=mesh,
        in_specs=(
            P(("row", "col")),
            P(("row", "col")),
            P(("row", "col"), None),
            P(("row", "col"), None),
            P(("row", "col"), None, None, None, None),
            P(("row", "col"), None, None, None, None),
            P(),
            P(),
            P(),
        ),
        out_specs=(P(("row", "col"), None), P(("row", "col"), None)),
        check_vma=False,
    )
```

time: 278 us -> 112 us (0.40)
  the two profiles are of different devices: /device:TPU:0 before, /device:TPU:4 now
where the time goes in v1:
time: 112 us
  Pallas kernels  108 us (96%)
  local copies, waits for them, and re-layouts  3.44 us (3%)
    pallas_call x1, Pallas kernels, local(): pl.pallas_call(parent_kernel, name='parent_side', out_shape=(jax.ShapeDty...  70.7 us
    pallas_call x1, Pallas kernels, local(): pl.pallas_call(prefix_kernel, name='prefix_side', out_shape=(jax.ShapeDty...  37.2 us

profile of v1, /device:TPU:4, one launch (start us, length us, event | category | flops | bytes accessed | tf_op | source)
XLA Modules:
  0.0 112.0 jit_solution(1389252449076214400)
XLA Ops:
  0.6 1.3 %reshape.18.gain_ref = f32[1,3584]{1,0:T(1,128)} reshape(f32[3584]{0:T(1024)} %param.15) | data formatting | bytes 28672 | tf_op jit(solution)/shard_map/reshape | solution.py:587
  2.0 0.0 copy-start
  2.0 0.0 copy-start.3
  2.0 0.0 copy-start.4
  2.0 70.7 %parent_side.1 = (bf16[3,128,768]{2,1,0:T(8,128)(2,1)}, bf16[2,128,1024]{2,1,0:T(8,128)(2,1)}) custom-call(s32[1,128]{1,0:T(1,128)} %bitcast.4, f32[1,3584]{1,0:T(1,128)} %reshape.18.gain_ref, bf16[128,3584]{1,0:T(8,128)(2,1)} %delta_hbm.1, bf16[32,3584]{1,0:T(8,128)(2,1)} %hidden_hbm.1, bf16[32,2,2,128,128]{4,3,2,1,0:T(8,128)(2,1)} %blocks_hbm.1, ...), custom_call_target="tpu_custom_call" | custom-call | tf_op jit(solution)/shard_map/parent_side/pallas_call | solution.py:531
  72.7 0.0 copy-done
  72.7 0.0 copy-done.3
  72.7 0.0 copy-done.4
  72.7 0.0 copy-start.1
  72.7 1.1 copy-done.1
  73.8 0.0 copy-start.2
  73.8 1.0 copy-done.2
  74.8 37.2 %prefix_side.1 = (bf16[128,1792]{1,0:T(8,128)(2,1)}, bf16[128,512]{1,0:T(8,128)(2,1)}) custom-call(s32[1,128]{1,0:T(1,128)S(1)} %bitcast.5, s32[1,128]{1,0:T(1,128)S(1)} %bitcast.6, bf16[3,128,768]{2,1,0:T(8,128)(2,1)S(1)} %copy-done.1, bf16[2,128,1024]{2,1,0:T(8,128)(2,1)S(1)} %copy-done.2, bf16[2,2,5120,128]{3,2,1,0:T(8,128)(2,1)S(1)} %bitcast.3), custom_call_target="tpu_custom_call" | custom-call | tf_op jit(solution)/shard_map/prefix_side/pallas_call | solution.py:589
Async XLA Ops:
  2.0 70.7 %copy-start = (bf16[1,2,2,5120,128]{4,3,2,1,0:T(8,128)(2,1)S(1)}, bf16[1,2,2,5120,128]{4,3,2,1,0:T(8,128)(2,1)}, u32[]{:S(2)}) copy-start(bf16[1,2,2,5120,128]{4,3,2,1,0:T(8,128)(2,1)} %param.14) | copy-start | bytes 15728644
  2.0 70.7 %copy-start.3 = (s32[128]{0:T(128)S(1)}, s32[128]{0:T(128)}, u32[]{:S(2)}) copy-start(s32[128]{0:T(128)} %param.9) | copy-start | bytes 1540
  2.0 70.7 %copy-start.4 = (s32[128]{0:T(128)S(1)}, s32[128]{0:T(128)}, u32[]{:S(2)}) copy-start(s32[128]{0:T(128)} %param.10) | copy-start | bytes 1540
  72.7 1.1 copy-start.1
  73.8 1.0 copy-start.2

commit v2 on v1

--- a/solution.py
+++ b/solution.py
@@ -1,4 +1,3 @@
-import functools
 import math
 
 import jax
@@ -26,8 +25,8 @@
 HALF = CHUNK // 2
 BACK_CHUNKS = 3
 SHARE_CHUNKS = 2
-TILE = 32
 KEYS = 512
+EXCLUDED = -1e30
 SCORE_SCALE = math.log2(math.e) / math.sqrt(DH)
 
 
@@ -112,16 +111,18 @@
         self.each(lambda k: self.copy(src, dst, send, recv, k, self.me).wait_send())
 
 
-def parent_kernel(
+def layer_kernel(
     ids_ref,
+    lens_ref,
     gain_ref,
     delta_hbm,
     hidden_hbm,
     blocks_hbm,
     wq_hbm,
     wkv_hbm,
-    back_ref,
-    share_ref,
+    prefix_hbm,
+    context_ref,
+    kv_ref,
     delta_v,
     hidden_v,
     blocks_v,
@@ -147,6 +148,14 @@
     share1,
     share1_in,
     share2,
+    back_in,
+    share_in,
+    prefix_v,
+    block_v,
+    query_v,
+    near_score,
+    near_total,
+    near_top,
     load_sem,
     d1s,
     d1r,
@@ -204,13 +213,24 @@
     local_sorted = jnp.sum(jnp.where(pick, far_local, 0.0), axis=1, keepdims=True)
     id_out1[...] = jnp.where(along < 64, row_sorted, local_sorted).astype(BF16)
 
-    load_delta.wait()
     loads = [
         pltpu.make_async_copy(hidden_hbm, hidden_v, load_sem.at[1]),
         pltpu.make_async_copy(wq_hbm, weight_v.at[:, pl.ds(0, HEADS * DH)], load_sem.at[2]),
         pltpu.make_async_copy(wkv_hbm, weight_v.at[:, pl.ds(HEADS * DH, 512)], load_sem.at[3]),
         pltpu.make_async_copy(blocks_hbm, blocks_v, load_sem.at[4]),
+        pltpu.make_async_copy(prefix_hbm, prefix_v, load_sem.at[5]),
     ]
+    load_delta.wait()
+    for load in loads:
+        load.start()
+    order_col = to_col(order)
+    unsort = one_zero(order_col == along.astype(F32))
+    lens_col = to_col(lens_ref[...].astype(F32))
+    bias = jnp.where(along.astype(F32) < lens_col, 0.0, EXCLUDED).astype(BF16)
+    for h in range(HEADS):
+        query_v[h, :, DH:] = bias
+    for b in range(prefix_v.shape[2] // BLOCK):
+        block_v[b * BLOCK : (b + 1) * BLOCK] = one_zero(along == b)
 
     by_col = Exchange("col", COLS, my_col, 16)
     by_row = Exchange("row", ROWS, my_row, 16)
@@ -221,8 +241,6 @@
     for c in range(DELTA_CHUNKS):
         out1[c] = dot(sorting, delta_v[:, c * CHUNK : (c + 1) * CHUNK]).astype(BF16)
         by_col.start(out1.at[c], in1.at[c], d1s.at[c], d1r.at[c])
-    for load in loads:
-        load.start()
 
     by_col.arrived(id_out1, id_in1, i1s, i1r)
     arrived_ids = id_in1[...].astype(F32)
@@ -274,7 +292,7 @@
     for w in range(D // 128):
         at = w * 128
         normed[:, at : at + 128] = (
-            wide[:, at : at + 128] * inverse * gain_ref[:, at : at + 128]
+            wide[:, at : at + 128] * inverse * gain_ref[w : w + 1]
         ).astype(BF16)
 
     loads[1].wait()
@@ -319,7 +337,7 @@
         for t in range(3):
             back2[c, :, t * 256 : t * 256 + 128] = turned[:N, t * 128 : (t + 1) * 128]
             back2[c, :, t * 256 + 128 : (t + 1) * 256] = turned[N:, t * 128 : (t + 1) * 128]
-        by_col.start(back2.at[c], back_ref.at[c], b2s.at[c], b2r.at[c])
+        by_col.start(back2.at[c], back_in.at[c], b2s.at[c], b2r.at[c])
 
     for g in range(2):
         stats = jnp.zeros((N, N), F32)
@@ -362,17 +380,85 @@
             share1[c, :, b * 128 : (b + 1) * 128] = pair_rows(sides[0], sides[1]).astype(BF16)
         by_row.start(share1.at[c], share1_in.at[c], s1s.at[c], s1r.at[c])
 
+    for c in range(BACK_CHUNKS):
+        by_col.arrived(back2.at[c], back_in.at[c], b2s.at[c], b2r.at[c])
+        own = dot(unsort, back_in[c]).astype(BF16)
+        for t in range(3):
+            n = c * 3 + t
+            if n < GROUP:
+                query_v[2 * n, :, :DH] = own[:, t * 256 : t * 256 + 128]
+                query_v[2 * n + 1, :, :DH] = own[:, t * 256 + 128 : (t + 1) * 256]
+            else:
+                kv_ref[:, (n - GROUP) * 256 : (n - GROUP + 1) * 256] = own[
+                    :, t * 256 : (t + 1) * 256
+                ]
+    loads[4].wait()
+    spans = [slice(k, k + KEYS) for k in range(0, prefix_v.shape[2], KEYS)]
+    ones = jnp.ones((KEYS, DH), BF16)
+
+    def near_scores(h, g, slot):
+        q = query_v[h]
+        top = jnp.full((N, DH), EXCLUDED, F32)
+        for span in spans:
+            keys = jnp.concatenate([prefix_v[0, g, span], block_v[span]], axis=1)
+            part = dot_t(q, keys)
+            near_score[slot, :, span] = part
+            for w in range(KEYS // 128):
+                top = jnp.maximum(top, part[:, w * 128 : (w + 1) * 128])
+        near_top[h] = jnp.broadcast_to(
+            jnp.max(top, axis=1, keepdims=True) * SCORE_SCALE, (N, DH)
+        )
+
+    def near_values(h, g, slot):
+        top = near_top[h][:, :1]
+        sums = jnp.zeros((N, 2 * DH), F32)
+        for span in spans:
+            e = jnp.exp2(near_score[slot, :, span] * SCORE_SCALE - top).astype(BF16)
+            sums = sums + dot(e, jnp.concatenate([prefix_v[1, g, span], ones], axis=1))
+        near_total[h] = sums
+
+    def head(h, carry):
+        later = (h + 1) % HEADS
+        near_scores(later, later // GROUP, (h + 1) % 2)
+        near_values(h, h // GROUP, h % 2)
+        return carry
+
+    near_scores(0, 0, 0)
+    lax.fori_loop(0, GROUP, head, 0)
+
     for c in range(SHARE_CHUNKS):
         by_row.arrived(share1.at[c], share1_in.at[c], s1s.at[c], s1r.at[c])
         turned = dot(turn, share1_in[c]).astype(BF16)
         share2[c, :, :512] = turned[:N]
         share2[c, :, 512:] = turned[N:]
-        by_col.start(share2.at[c], share_ref.at[c], s2s.at[c], s2r.at[c])
-
-    for c in range(BACK_CHUNKS):
-        by_col.arrived(back2.at[c], back_ref.at[c], b2s.at[c], b2r.at[c])
+        by_col.start(share2.at[c], share_in.at[c], s2s.at[c], s2r.at[c])
+
+    lax.fori_loop(GROUP, HEADS, head, 0)
+
     for c in range(SHARE_CHUNKS):
-        by_col.arrived(share2.at[c], share_ref.at[c], s2s.at[c], s2r.at[c])
+        by_col.arrived(share2.at[c], share_in.at[c], s2s.at[c], s2r.at[c])
+    for g in range(2):
+        packed = dot(unsort, share_in[1, :, g * 512 + 384 : g * 512 + 512])
+        stats = (
+            packed
+            + pltpu.roll(packed, shift=N - 16, axis=1)
+            + pltpu.roll(packed, shift=N - 32, axis=1)
+        )
+        for h in range(GROUP):
+            c, b = h // 4, h % 4
+            i = g * GROUP + h
+            part = dot(unsort, share_in[c, :, g * 512 + b * 128 : g * 512 + (b + 1) * 128])
+            top_far = stats[:, h : h + 1]
+            mass_far = stats[:, 8 + h : 9 + h]
+            top_near = near_top[i]
+            top = jnp.maximum(top_near, top_far)
+            near = jnp.exp2(top_near - top)
+            far = jnp.exp2(top_far - top) * mass_far
+            sums = near_total[i]
+            whole = sums[:, DH:] * near + far
+            context_ref[:, i * DH : (i + 1) * DH] = (
+                (sums[:, :DH] * near + part * far) / whole
+            ).astype(BF16)
 
     by_col.sent(id_out1, id_in1, i1s, i1r)
     by_row8.sent(id_out2, id_in2, i2s, i2r)
@@ -381,133 +467,10 @@
         by_row.sent(out2.at[c], in2.at[c], d2s.at[c], d2r.at[c])
     for c in range(BACK_CHUNKS):
         by_row.sent(back1.at[c], back1_in.at[c], b1s.at[c], b1r.at[c])
-        by_col.sent(back2.at[c], back_ref.at[c], b2s.at[c], b2r.at[c])
+        by_col.sent(back2.at[c], back_in.at[c], b2s.at[c], b2r.at[c])
     for c in range(SHARE_CHUNKS):
         by_row.sent(share1.at[c], share1_in.at[c], s1s.at[c], s1r.at[c])
-        by_col.sent(share2.at[c], share_ref.at[c], s2s.at[c], s2r.at[c])
-
-
-def prefix_kernel(
-    ids_ref,
-    lens_ref,
-    back_ref,
-    share_ref,
-    prefix_hbm,
-    context_ref,
-    kv_ref,
-    keys_v,
-    values_v,
-    query_v,
-    part_v,
-    stat_v,
-    result_v,
-    top,
-    mass,
-    total,
-    load_sem,
-):
-    loads = []
-    for g in range(2):
-        loads.append(
-            pltpu.make_async_copy(prefix_hbm.at[0, g], keys_v.at[g], load_sem.at[2 * g])
-        )
-        loads.append(
-            pltpu.make_async_copy(prefix_hbm.at[1, g], values_v.at[g], load_sem.at[2 * g + 1])
-        )
-    for load in loads:
-        load.start()
-
-    below, along = iotas((N, N))
-    along_f = along.astype(F32)
-    below_f = below.astype(F32)
-    arrive_col = to_col(column_order(ids_ref[...]))
-    lens = lens_ref[...].astype(F32)
-    lens_col = to_col(lens)
-    before = (lens_col > lens) | ((lens_col == lens) & (below < along))
-    place = jnp.sum(jnp.where(before, 1.0, 0.0), axis=0, keepdims=True)
-    place_col = to_col(place)
-    unsort1 = one_zero(arrive_col == along_f)
-    pick = place == below_f
-    gather = dot(one_zero(pick), unsort1).astype(BF16)
-    sorted_lens = jnp.sum(jnp.where(pick, lens, 0.0), axis=1, keepdims=True)
-
-    for n in range(GROUP):
-        c, t = n // 3, n % 3
-        query_v[:, n * 256 : (n + 1) * 256] = dot(
-            gather, back_ref[c, :, t * 256 : (t + 1) * 256]
-        ).astype(BF16)
-    for n in range(2):
-        kv_ref[:, n * 256 : (n + 1) * 256] = dot(
-            unsort1, back_ref[2, :, (n + 1) * 256 : (n + 2) * 256]
-        ).astype(BF16)
-    for g in range(2):
-        for h in range(GROUP):
-            c, b = h // 4, h % 4
-            part_v[:, (g * GROUP + h) * 128 : (g * GROUP + h + 1) * 128] = dot(
-                gather, share_ref[c, :, g * 512 + b * 128 : g * 512 + (b + 1) * 128]
-            )
-        packed = dot(gather, share_ref[1, :, g * 512 + 384 : g * 512 + 512])
-        stat_v[g] = (
-            packed
-            + pltpu.roll(packed, shift=N - 16, axis=1)
-            + pltpu.roll(packed, shift=N - 32, axis=1)
-        )
-
-    for g in range(2):
-        loads[2 * g].wait()
-        loads[2 * g + 1].wait()
-        for t in range(N // TILE):
-            rows = slice(t * TILE, (t + 1) * TILE)
-            limit = jnp.concatenate([sorted_lens[rows] * float(BLOCK)] * GROUP, axis=0)
-            longest = jnp.max(sorted_lens[rows]).astype(I32)
-            steps = (longest * BLOCK + KEYS - 1) // KEYS
-            q = jnp.concatenate(
-                [
-                    query_v[rows, (g * GROUP + h) * 128 : (g * GROUP + h + 1) * 128]
-                    for h in range(GROUP)
-                ],
-                axis=0,
-            )
-            top[...] = jnp.full_like(top, -jnp.inf)
-            mass[...] = jnp.zeros_like(mass)
-            total[...] = jnp.zeros_like(total)
-
-            def step(j, carry, g=g, q=q, limit=limit):
-                start = pl.multiple_of(j * KEYS, KEYS)
-                s = dot_t(q, keys_v[g, pl.ds(start, KEYS), :]) * SCORE_SCALE
-                spot = lax.broadcasted_iota(I32, s.shape, 1).astype(F32) + start.astype(F32)
-                s = jnp.where(spot < limit, s, -jnp.inf)
-                old = top[...]
-                new = jnp.maximum(old, jnp.max(s, axis=1, keepdims=True))
-                p = jnp.exp2(s - new)
-                shrink = jnp.exp2(old - new)
-                mass[...] = mass[...] * shrink + jnp.sum(p, axis=1, keepdims=True)
-                total[...] = total[...] * shrink + dot(
-                    p.astype(BF16), values_v[g, pl.ds(start, KEYS), :]
-                )
-                top[...] = new
-                return carry
-
-            lax.fori_loop(0, steps, step, 0)
-            stats = stat_v[g, rows]
-            for h in range(GROUP):
-                at = (g * GROUP + h) * 128
-                own = slice(h * TILE, (h + 1) * TILE)
-                top_par = stats[:, h : h + 1]
-                mass_par = stats[:, 8 + h : 9 + h]
-                top_all = jnp.maximum(top[own], top_par)
-                near = jnp.exp2(top[own] - top_all)
-                far = jnp.exp2(top_par - top_all) * mass_par
-                whole = mass[own] * near + far
-                result_v[rows, at : at + 128] = (
-                    (total[own] * near + part_v[rows, at : at + 128] * far) / whole
-                ).astype(BF16)
-
-    unsort = one_zero(place_col == along_f)
-    for n in range(GROUP):
-        context_ref[:, n * 256 : (n + 1) * 256] = dot(
-            unsort, result_v[:, n * 256 : (n + 1) * 256]
-        ).astype(BF16)
+        by_col.sent(share2.at[c], share_in.at[c], s2s.at[c], s2r.at[c])
 
 
 def local(
@@ -526,16 +489,17 @@
     dma = pltpu.SemaphoreType.DMA
     ids = child_parent.reshape(1, N)
     lens = prefix_len.reshape(1, N)
+    tokens = prefix_cache.shape[3]
     back_shape = (BACK_CHUNKS, N, 768)
     share_shape = (SHARE_CHUNKS, N, 1024)
-    back, share = pl.pallas_call(
-        parent_kernel,
-        name="parent_side",
+    return pl.pallas_call(
+        layer_kernel,
+        name="decode_layer",
         out_shape=(
-            jax.ShapeDtypeStruct(back_shape, BF16),
-            jax.ShapeDtypeStruct(share_shape, BF16),
+            jax.ShapeDtypeStruct((N, HEADS * DH), BF16),
+            jax.ShapeDtypeStruct((N, 512), BF16),
         ),
-        in_specs=[vmem, vmem, hbm, hbm, hbm, hbm, hbm],
+        in_specs=[vmem, vmem, vmem, hbm, hbm, hbm, hbm, hbm, hbm],
         out_specs=(vmem, vmem),
         scratch_shapes=[
             pltpu.VMEM((N, D), BF16),
@@ -563,7 +527,15 @@
             pltpu.VMEM((SHARE_CHUNKS, 2 * N, 512), BF16),
             pltpu.VMEM((SHARE_CHUNKS, 2 * N, 512), BF16),
             pltpu.VMEM(share_shape, BF16),
-            dma((5,)),
+            pltpu.VMEM(back_shape, BF16),
+            pltpu.VMEM(share_shape, BF16),
+            pltpu.VMEM((2, 2, tokens, DH), BF16),
+            pltpu.VMEM((tokens, BLOCK), BF16),
+            pltpu.VMEM((HEADS, N, 2 * DH), BF16),
+            pltpu.VMEM((2, N, tokens), F32),
+            pltpu.VMEM((HEADS, N, 2 * DH), F32),
+            pltpu.VMEM((HEADS, N, DH), F32),
+            dma((6,)),
             dma((DELTA_CHUNKS, COLS)),
             dma((DELTA_CHUNKS, COLS)),
             dma((DELTA_CHUNKS, ROWS)),
@@ -582,34 +554,19 @@
             dma((SHARE_CHUNKS, COLS)),
         ],
         compiler_params=pltpu.CompilerParams(
-            collective_id=0, has_side_effects=True, vmem_limit_bytes=56 << 20
+            collective_id=0, has_side_effects=True, vmem_limit_bytes=60 << 20
         ),
-    )(ids, norm_gain.reshape(1, D), child_delta, parent_hidden, parent_cache, w_query, w_kv)
-    tokens = prefix_cache.shape[3]
-    context, new_kv = pl.pallas_call(
-        prefix_kernel,
-        name="prefix_side",
-        out_shape=(
-            jax.ShapeDtypeStruct((N, HEADS * DH), BF16),
-            jax.ShapeDtypeStruct((N, 512), BF16),
-        ),
-        in_specs=[vmem, vmem, vmem, vmem, hbm],
-        out_specs=(vmem, vmem),
-        scratch_shapes=[
-            pltpu.VMEM((2, tokens, DH), BF16),
-            pltpu.VMEM((2, tokens, DH), BF16),
-            pltpu.VMEM((N, HEADS * DH), BF16),
-            pltpu.VMEM((N, HEADS * DH), F32),
-            pltpu.VMEM((2, N, N), F32),
-            pltpu.VMEM((N, HEADS * DH), BF16),
-            pltpu.VMEM((GROUP * TILE, 1), F32),
-            pltpu.VMEM((GROUP * TILE, 1), F32),
-            pltpu.VMEM((GROUP * TILE, DH), F32),
-            dma((4,)),
-        ],
-        compiler_params=pltpu.CompilerParams(vmem_limit_bytes=40 << 20),
-    )(ids, lens, back, share, prefix_cache.reshape(prefix_cache.shape[1:]))
-    return context, new_kv
+    )(
+        ids,
+        lens,
+        norm_gain.reshape(D // 128, 128),
+        child_delta,
+        parent_hidden,
+        parent_cache,
+        w_query,
+        w_kv,
+        prefix_cache.reshape(prefix_cache.shape[1:]),
+    )
 
 
 def solution(mesh):

time: 112 us -> 96.6 us (0.86)
  the two profiles are of different devices: /device:TPU:4 before, /device:TPU:0 now
where the time goes in v2:
time: 96.6 us; the launch traced here: 96.3 us
  Pallas kernels  92.2 us (95%)
  local copies, waits for them, and re-layouts  3.38 us (3%)
    pallas_call x1, Pallas kernels, local(): pl.pallas_call(layer_kernel, name='decode_layer', out_shape=(jax.ShapeDty...  92.2 us
    unnamed x2, local copies, waits for them, and re-layouts  3.38 us

profile of v2, /device:TPU:0, one launch (start us, length us, event | category | flops | bytes accessed | tf_op | source)
XLA Modules:
  0.0 96.3 jit_solution(14329084236037446135)
XLA Ops:
  0.6 92.2 %decode_layer.1 = (bf16[128,1792]{1,0:T(8,128)(2,1)}, bf16[128,512]{1,0:T(8,128)(2,1)}) custom-call(s32[1,128]{1,0:T(1,128)} %bitcast.6, s32[1,128]{1,0:T(1,128)} %bitcast.7, f32[28,128]{1,0:T(8,128)} %bitcast.5, bf16[128,3584]{1,0:T(8,128)(2,1)} %delta_hbm.1, bf16[32,3584]{1,0:T(8,128)(2,1)} %hidden_hbm.1, bf16[32,2,2,128,128]{4,3,2,1,0:T(8,128)(2,1)} %blocks_hbm.1, ...), custom_call_target="tpu_custom_call" | custom-call | tf_op jit(solution)/shard_map/decode_layer/pallas_call | solution.py:495
  92.9 1.8 %copy.13 = bf16[128,1792]{1,0:T(8,128)(2,1)} copy(bf16[128,1792]{1,0:T(8,128)(2,1)} %get-tuple-element.4) | data formatting | bytes 917504
  94.7 1.6 %copy.14 = bf16[128,512]{1,0:T(8,128)(2,1)} copy(bf16[128,512]{1,0:T(8,128)(2,1)} %get-tuple-element.5) | data formatting | bytes 262144

commit v3 on v2

--- a/solution.py
+++ b/solution.py
@@ -26,6 +26,10 @@
 BACK_CHUNKS = 3
 SHARE_CHUNKS = 2
 KEYS = 512
+TILES = 4
+TILE = GROUP * N * 2 // TILES
+OCTET = 8
+SIDE = N // 2
 EXCLUDED = -1e30
 SCORE_SCALE = math.log2(math.e) / math.sqrt(DH)
 
@@ -135,14 +139,11 @@
     id_in1,
     id_out2,
     id_in2,
-    wide,
     normed,
     heads_v,
     back1,
     back1_in,
     back2,
-    score,
-    total,
     prob,
     stat,
     share1,
@@ -227,8 +228,16 @@
     unsort = one_zero(order_col == along.astype(F32))
     lens_col = to_col(lens_ref[...].astype(F32))
     bias = jnp.where(along.astype(F32) < lens_col, 0.0, EXCLUDED).astype(BF16)
+
+    def store_query(h, lanes, value):
+        at = (h % GROUP) * SIDE
+        for side in range(2):
+            query_v[(h // GROUP) * 2 + side, at : at + SIDE, lanes] = value[
+                side * SIDE : (side + 1) * SIDE
+            ]
+
     for h in range(HEADS):
-        query_v[h, :, DH:] = bias
+        store_query(h, slice(DH, 2 * DH), bias)
     for b in range(prefix_v.shape[2] // BLOCK):
         block_v[b * BLOCK : (b + 1) * BLOCK] = one_zero(along == b)
 
@@ -236,6 +245,11 @@
     by_row = Exchange("row", ROWS, my_row, 16)
     by_row8 = Exchange("row", ROWS, my_row, 8)
 
+    wide = near_score.at[0:N, 0:D]
+    score = near_score.at[N : 2 * N, 0 : HEADS * DH]
+    total = near_score.at[2 * N : 3 * N, 0 : HEADS * DH]
+    score[...] = jnp.zeros(score.shape, F32)
+    total[...] = jnp.zeros(total.shape, F32)
     pl.semaphore_wait(barrier, COLS + ROWS - 2)
     by_col.start(id_out1, id_in1, i1s, i1r)
     for c in range(DELTA_CHUNKS):
@@ -313,25 +327,8 @@
         by_row.start(back1.at[c], back1_in.at[c], b1s.at[c], b1r.at[c])
 
     loads[3].wait()
-    score[...] = jnp.zeros_like(score)
-    total[...] = jnp.zeros_like(total)
-
-    def masks(k):
-        first = (2 * k).astype(F32)
-        return one_zero(local_id == first), one_zero(local_id == first + 1.0)
-
-    def score_pair(k, carry):
-        mask0, mask1 = masks(k)
-        for g in range(2):
-            keys = jnp.concatenate([blocks_v[2 * k, 0, g], blocks_v[2 * k + 1, 0, g]], axis=1)
-            for h in range(g * GROUP, (g + 1) * GROUP):
-                q = heads_v[h]
-                score[h] += dot_t(jnp.concatenate([q * mask0, q * mask1], axis=1), keys)
-        return carry
-
-    lax.fori_loop(0, PARENTS // 2, score_pair, 0)
-
-    for c in range(BACK_CHUNKS):
+
+    def pass_back(c):
         by_row.arrived(back1.at[c], back1_in.at[c], b1s.at[c], b1r.at[c])
         turned = dot(turn, back1_in[c]).astype(BF16)
         for t in range(3):
@@ -339,10 +336,47 @@
             back2[c, :, t * 256 + 128 : (t + 1) * 256] = turned[N:, t * 128 : (t + 1) * 128]
         by_col.start(back2.at[c], back_in.at[c], b2s.at[c], b2r.at[c])
 
+    def masked(source, g, masks):
+        return jnp.concatenate(
+            [
+                jnp.concatenate([source[g * GROUP + h] * mask for mask in masks], axis=1)
+                for h in range(GROUP)
+            ],
+            axis=0,
+        )
+
+    def masks_of(k):
+        return [one_zero(local_id == (OCTET * k + i).astype(F32)) for i in range(OCTET)]
+
+    def add_heads(target, g, value):
+        for h in range(GROUP):
+            at = (g * GROUP + h) * DH
+            target[:, at : at + DH] += value[h * N : (h + 1) * N]
+
+    def score_octet(k, carry):
+        masks = masks_of(k)
+        for g in range(2):
+            keys = jnp.concatenate([blocks_v[OCTET * k + i, 0, g] for i in range(OCTET)], axis=1)
+            add_heads(score, g, dot_t(masked(heads_v, g, masks), keys))
+        return carry
+
+    def value_octet(k, carry):
+        masks = masks_of(k)
+        for g in range(2):
+            values = jnp.concatenate([blocks_v[OCTET * k + i, 1, g] for i in range(OCTET)], axis=0)
+            add_heads(total, g, dot(masked(prob, g, masks), values))
+        return carry
+
+    lax.fori_loop(0, 2, score_octet, 0)
+    pass_back(0)
+    lax.fori_loop(2, 4, score_octet, 0)
+    pass_back(1)
+
     for g in range(2):
         stats = jnp.zeros((N, N), F32)
         for h in range(GROUP):
-            s = score[g * GROUP + h] * SCORE_SCALE
+            at = (g * GROUP + h) * DH
+            s = score[:, at : at + DH] * SCORE_SCALE
             top = jnp.max(s, axis=1, keepdims=True)
             e = jnp.exp2(s - top)
             prob[g * GROUP + h] = e.astype(BF16)
@@ -350,16 +384,9 @@
             stats = jnp.where(along == 8 + h, jnp.sum(e, axis=1, keepdims=True), stats)
         stat[g] = stats
 
-    def value_pair(k, carry):
-        mask0, mask1 = masks(k)
-        for g in range(2):
-            values = jnp.concatenate([blocks_v[2 * k, 1, g], blocks_v[2 * k + 1, 1, g]], axis=0)
-            for h in range(g * GROUP, (g + 1) * GROUP):
-                p = prob[h]
-                total[h] += dot(jnp.concatenate([p * mask0, p * mask1], axis=1), values)
-        return carry
-
-    lax.fori_loop(0, PARENTS // 2, value_pair, 0)
+    lax.fori_loop(0, 2, value_octet, 0)
+    pass_back(2)
+    lax.fori_loop(2, 4, value_octet, 0)
 
     for c in range(SHARE_CHUNKS):
         for b in range(4):
@@ -368,7 +395,8 @@
             for g in range(2):
                 stats = stat[g]
                 if h < GROUP:
-                    sides.append(total[g * GROUP + h] / stats[:, 8 + h : 9 + h])
+                    at = (g * GROUP + h) * DH
+                    sides.append(total[:, at : at + DH] / stats[:, 8 + h : 9 + h])
                 else:
                     high = stats.astype(BF16).astype(F32)
                     rest = stats - high
@@ -386,8 +414,8 @@
         for t in range(3):
             n = c * 3 + t
             if n < GROUP:
-                query_v[2 * n, :, :DH] = own[:, t * 256 : t * 256 + 128]
-                query_v[2 * n + 1, :, :DH] = own[:, t * 256 + 128 : (t + 1) * 256]
+                for half in range(2):
+                    store_query(2 * n + half, slice(0, DH), own[:, t * 256 + half * 128 :][:, :DH])
             else:
                 kv_ref[:, (n - GROUP) * 256 : (n - GROUP + 1) * 256] = own[
                     :, t * 256 : (t + 1) * 256
@@ -396,35 +424,41 @@
     spans = [slice(k, k + KEYS) for k in range(0, prefix_v.shape[2], KEYS)]
     ones = jnp.ones((KEYS, DH), BF16)
 
-    def near_scores(h, g, slot):
-        q = query_v[h]
-        top = jnp.full((N, DH), EXCLUDED, F32)
+    def near_scores(q, g, span, top):
+        keys = jnp.concatenate([prefix_v[0, g, span], block_v[span]], axis=1)
+        part = dot_t(q, keys)
+        near_score[:, span] = part
+        for w in range(KEYS // 128):
+            top = jnp.maximum(top, part[:, w * 128 : (w + 1) * 128])
+        return top
+
+    def near_values(top, g, span, sums):
+        e = jnp.exp2(near_score[:, span] * SCORE_SCALE - top).astype(BF16)
+        return sums + dot(e, jnp.concatenate([prefix_v[1, g, span], ones], axis=1))
+
+    def keep_top(t, top):
+        near_top[t] = jnp.broadcast_to(
+            jnp.max(top, axis=1, keepdims=True) * SCORE_SCALE, (TILE, DH)
+        )
+
+    def tile(t, carry):
+        later = t + 1
+        q = query_v[later]
+        top = near_top[t][:, :1]
+        next_top = jnp.full((TILE, DH), EXCLUDED, F32)
+        sums = jnp.zeros((TILE, 2 * DH), F32)
         for span in spans:
-            keys = jnp.concatenate([prefix_v[0, g, span], block_v[span]], axis=1)
-            part = dot_t(q, keys)
-            near_score[slot, :, span] = part
-            for w in range(KEYS // 128):
-                top = jnp.maximum(top, part[:, w * 128 : (w + 1) * 128])
-        near_top[h] = jnp.broadcast_to(
-            jnp.max(top, axis=1, keepdims=True) * SCORE_SCALE, (N, DH)
-        )
-
-    def near_values(h, g, slot):
-        top = near_top[h][:, :1]
-        sums = jnp.zeros((N, 2 * DH), F32)
-        for span in spans:
-            e = jnp.exp2(near_score[slot, :, span] * SCORE_SCALE - top).astype(BF16)
-            sums = sums + dot(e, jnp.concatenate([prefix_v[1, g, span], ones], axis=1))
-        near_total[h] = sums
-
-    def head(h, carry):
-        later = (h + 1) % HEADS
-        near_scores(later, later // GROUP, (h + 1) % 2)
-        near_values(h, h // GROUP, h % 2)
+            sums = near_values(top, t // 2, span, sums)
+            next_top = near_scores(q, later // 2, span, next_top)
+        near_total[t] = sums
+        keep_top(later, next_top)
         return carry
 
-    near_scores(0, 0, 0)
-    lax.fori_loop(0, GROUP, head, 0)
+    first_top = jnp.full((TILE, DH), EXCLUDED, F32)
+    for span in spans:
+        first_top = near_scores(query_v[0], 0, span, first_top)
+    keep_top(0, first_top)
+    lax.fori_loop(0, TILES // 2, tile, 0)
 
     for c in range(SHARE_CHUNKS):
         by_row.arrived(share1.at[c], share1_in.at[c], s1s.at[c], s1r.at[c])
@@ -433,7 +467,12 @@
         share2[c, :, 512:] = turned[N:]
         by_col.start(share2.at[c], share_in.at[c], s2s.at[c], s2r.at[c])
 
-    lax.fori_loop(GROUP, HEADS, head, 0)
+    lax.fori_loop(TILES // 2, TILES - 1, tile, 0)
+    last_top = near_top[TILES - 1][:, :1]
+    last_sums = jnp.zeros((TILE, 2 * DH), F32)
+    for span in spans:
+        last_sums = near_values(last_top, 1, span, last_sums)
+    near_total[TILES - 1] = last_sums
 
     for c in range(SHARE_CHUNKS):
         by_col.arrived(share2.at[c], share_in.at[c], s2s.at[c], s2r.at[c])
@@ -450,11 +489,12 @@
             part = dot(unsort, share_in[c, :, g * 512 + b * 128 : g * 512 + (b + 1) * 128])
             top_far = stats[:, h : h + 1]
             mass_far = stats[:, 8 + h : 9 + h]
-            top_near = near_top[i]
+            rows = slice(h * SIDE, (h + 1) * SIDE)
+            top_near = jnp.concatenate([near_top[2 * g, rows], near_top[2 * g + 1, rows]], axis=0)
             top = jnp.maximum(top_near, top_far)
             near = jnp.exp2(top_near - top)
             far = jnp.exp2(top_far - top) * mass_far
-            sums = near_total[i]
+            sums = jnp.concatenate([near_total[2 * g, rows], near_total[2 * g + 1, rows]], axis=0)
             whole = sums[:, DH:] * near + far
             context_ref[:, i * DH : (i + 1) * DH] = (
                 (sums[:, :DH] * near + part * far) / whole
@@ -514,14 +554,11 @@
             pltpu.VMEM((N, N), BF16),
             pltpu.VMEM((N, N), F32),
             pltpu.VMEM((N, N), F32),
-            pltpu.VMEM((N, D), F32),
             pltpu.VMEM((N, D), BF16),
             pltpu.VMEM((18, N, 128), BF16),
             pltpu.VMEM((BACK_CHUNKS, 2 * N, 384), BF16),
             pltpu.VMEM((BACK_CHUNKS, 2 * N, 384), BF16),
             pltpu.VMEM(back_shape, BF16),
-            pltpu.VMEM((HEADS, N, BLOCK), F32),
-            pltpu.VMEM((HEADS, N, DH), F32),
             pltpu.VMEM((HEADS, N, BLOCK), BF16),
             pltpu.VMEM((2, N, N), F32),
             pltpu.VMEM((SHARE_CHUNKS, 2 * N, 512), BF16),
@@ -531,10 +568,10 @@
             pltpu.VMEM(share_shape, BF16),
             pltpu.VMEM((2, 2, tokens, DH), BF16),
             pltpu.VMEM((tokens, BLOCK), BF16),
-            pltpu.VMEM((HEADS, N, 2 * DH), BF16),
-            pltpu.VMEM((2, N, tokens), F32),
-            pltpu.VMEM((HEADS, N, 2 * DH), F32),
-            pltpu.VMEM((HEADS, N, DH), F32),
+            pltpu.VMEM((TILES, TILE, 2 * DH), BF16),
+            pltpu.VMEM((TILE, tokens), F32),
+            pltpu.VMEM((TILES, TILE, 2 * DH), F32),
+            pltpu.VMEM((TILES, TILE, DH), F32),
             dma((6,)),
             dma((DELTA_CHUNKS, COLS)),
             dma((DELTA_CHUNKS, COLS)),

time: 96.6 us -> 78.5 us (0.81)
  the two profiles are of different devices: /device:TPU:0 before, /device:TPU:9 now
where the time goes in v3:
time: 78.5 us; the launch traced here: 78.2 us
  Pallas kernels  74.2 us (95%)
  local copies, waits for them, and re-layouts  3.38 us (4%)
    pallas_call x1, Pallas kernels, local(): pl.pallas_call(layer_kernel, name='decode_layer', out_shape=(jax.ShapeDty...  74.2 us
    unnamed x2, local copies, waits for them, and re-layouts  3.38 us

profile of v3, /device:TPU:9, one launch (start us, length us, event | category | flops | bytes accessed | tf_op | source)
XLA Modules:
  0.0 78.2 jit_solution(8993030089054754577)
XLA Ops:
  0.6 74.2 %decode_layer.1 = (bf16[128,1792]{1,0:T(8,128)(2,1)}, bf16[128,512]{1,0:T(8,128)(2,1)}) custom-call(s32[1,128]{1,0:T(1,128)} %bitcast.6, s32[1,128]{1,0:T(1,128)} %bitcast.7, f32[28,128]{1,0:T(8,128)} %bitcast.5, bf16[128,3584]{1,0:T(8,128)(2,1)} %delta_hbm.1, bf16[32,3584]{1,0:T(8,128)(2,1)} %hidden_hbm.1, bf16[32,2,2,128,128]{4,3,2,1,0:T(8,128)(2,1)} %blocks_hbm.1, ...), custom_call_target="tpu_custom_call" | custom-call | tf_op jit(solution)/shard_map/decode_layer/pallas_call | solution.py:535
  74.8 1.8 %copy.13 = bf16[128,1792]{1,0:T(8,128)(2,1)} copy(bf16[128,1792]{1,0:T(8,128)(2,1)} %get-tuple-element.4) | data formatting | bytes 917504
  76.6 1.6 %copy.14 = bf16[128,512]{1,0:T(8,128)(2,1)} copy(bf16[128,512]{1,0:T(8,128)(2,1)} %get-tuple-element.5) | data formatting | bytes 262144

commit v4 on v3

--- a/solution.py
+++ b/solution.py
@@ -20,15 +20,17 @@
 DH = 128
 PARENTS = 32
 BLOCK = 128
-DELTA_CHUNKS = 2
-CHUNK = D // DELTA_CHUNKS
-HALF = CHUNK // 2
+DELTA_HALVES = (512, 512, 384, 384)
+DELTA_STARTS = (0, 1024, 2048, 2816)
+DELTA_CHUNKS = 4
+BACK_TILES = (4, 3, 2)
+BACK_STARTS = (0, 4, 7)
 BACK_CHUNKS = 3
 SHARE_CHUNKS = 2
 KEYS = 512
 TILES = 4
 TILE = GROUP * N * 2 // TILES
-OCTET = 8
+PAIRS = 8
 SIDE = N // 2
 EXCLUDED = -1e30
 SCORE_SCALE = math.log2(math.e) / math.sqrt(DH)
@@ -157,6 +159,9 @@
     near_score,
     near_total,
     near_top,
+    kv_v,
+    context_v,
+    save_sem,
     load_sem,
     d1s,
     d1r,
@@ -229,6 +234,22 @@
     lens_col = to_col(lens_ref[...].astype(F32))
     bias = jnp.where(along.astype(F32) < lens_col, 0.0, EXCLUDED).astype(BF16)
 
+    by_col = Exchange("col", COLS, my_col, 16)
+    by_row = Exchange("row", ROWS, my_row, 16)
+    by_row8 = Exchange("row", ROWS, my_row, 8)
+
+    pl.semaphore_wait(barrier, COLS + ROWS - 2)
+    by_col.start(id_out1, id_in1, i1s, i1r)
+    for c in range(DELTA_CHUNKS):
+        first = DELTA_STARTS[c]
+        out1[c][...] = dot(sorting, delta_v[:, first : first + 2 * DELTA_HALVES[c]]).astype(BF16)
+        by_col.start(out1[c], in1[c], d1s.at[c], d1r.at[c])
+
+    wide = near_score.at[0:N, 0:D]
+    score = near_score.at[N : 2 * N, 0 : 2 * HEADS * DH]
+    total = near_score.at[2 * N : 3 * N, 0 : 2 * HEADS * DH]
+    score[...] = jnp.zeros(score.shape, F32)
+    total[...] = jnp.zeros(total.shape, F32)
     def store_query(h, lanes, value):
         at = (h % GROUP) * SIDE
         for side in range(2):
@@ -240,21 +261,6 @@
         store_query(h, slice(DH, 2 * DH), bias)
     for b in range(prefix_v.shape[2] // BLOCK):
         block_v[b * BLOCK : (b + 1) * BLOCK] = one_zero(along == b)
-
-    by_col = Exchange("col", COLS, my_col, 16)
-    by_row = Exchange("row", ROWS, my_row, 16)
-    by_row8 = Exchange("row", ROWS, my_row, 8)
-
-    wide = near_score.at[0:N, 0:D]
-    score = near_score.at[N : 2 * N, 0 : HEADS * DH]
-    total = near_score.at[2 * N : 3 * N, 0 : HEADS * DH]
-    score[...] = jnp.zeros(score.shape, F32)
-    total[...] = jnp.zeros(total.shape, F32)
-    pl.semaphore_wait(barrier, COLS + ROWS - 2)
-    by_col.start(id_out1, id_in1, i1s, i1r)
-    for c in range(DELTA_CHUNKS):
-        out1[c] = dot(sorting, delta_v[:, c * CHUNK : (c + 1) * CHUNK]).astype(BF16)
-        by_col.start(out1.at[c], in1.at[c], d1s.at[c], d1r.at[c])
 
     by_col.arrived(id_out1, id_in1, i1s, i1r)
     arrived_ids = id_in1[...].astype(F32)
@@ -282,10 +288,11 @@
     turn = one_zero(code_along == code_col)
 
     for c in range(DELTA_CHUNKS):
-        by_col.arrived(out1.at[c], in1.at[c], d1s.at[c], d1r.at[c])
-        stacked = jnp.concatenate([in1[c, :, :HALF], in1[c, :, HALF:]], axis=0)
-        out2[c] = dot(forth, stacked).astype(BF16)
-        by_row.start(out2.at[c], in2.at[c], d2s.at[c], d2r.at[c])
+        by_col.arrived(out1[c], in1[c], d1s.at[c], d1r.at[c])
+        width = DELTA_HALVES[c]
+        stacked = jnp.concatenate([in1[c][:, :width], in1[c][:, width:]], axis=0)
+        out2[c][...] = dot(forth, stacked).astype(BF16)
+        by_row.start(out2[c], in2[c], d2s.at[c], d2r.at[c])
 
     loads[0].wait()
     by_row8.arrived(id_out2, id_in2, i2s, i2r)
@@ -293,11 +300,11 @@
     owner = one_zero(local_id[:, :PARENTS] == along[:, :PARENTS].astype(F32))
     squares = jnp.zeros((N, 1), F32)
     for c in range(DELTA_CHUNKS):
-        by_row.arrived(out2.at[c], in2.at[c], d2s.at[c], d2r.at[c])
+        by_row.arrived(out2[c], in2[c], d2s.at[c], d2r.at[c])
         for half in range(2):
-            for w in range(HALF // 128):
-                at = c * CHUNK + half * HALF + w * 128
-                grid = in2[c, :, w * 128 : (w + 1) * 128].astype(F32)
+            for w in range(DELTA_HALVES[c] // 128):
+                at = DELTA_STARTS[c] + half * DELTA_HALVES[c] + w * 128
+                grid = in2[c][:, w * 128 : (w + 1) * 128].astype(F32)
                 grid = grid.reshape(ROWS, 2, 8, 128)[:, half].reshape(N, 128)
                 value = dot(owner, hidden_v[:, at : at + 128]) + grid
                 wide[:, at : at + 128] = value
@@ -314,27 +321,27 @@
     for c in range(BACK_CHUNKS):
 
         def project(t, carry, c=c):
-            n = c * 3 + t
+            n = BACK_STARTS[c] + t
             y = dot(normed[...], weight_v[:, pl.ds(pl.multiple_of(n * 256, 256), 256)])
             heads_v[2 * n] = y[:, :128].astype(BF16)
             heads_v[2 * n + 1] = y[:, 128:].astype(BF16)
-            back1[c, :, pl.ds(pl.multiple_of(t * 128, 128), 128)] = pair_rows(
+            back1[c][:, pl.ds(pl.multiple_of(t * 128, 128), 128)] = pair_rows(
                 y[:, :128], y[:, 128:]
             ).astype(BF16)
             return carry
 
-        lax.fori_loop(0, 3, project, 0)
-        by_row.start(back1.at[c], back1_in.at[c], b1s.at[c], b1r.at[c])
+        lax.fori_loop(0, BACK_TILES[c], project, 0)
+        by_row.start(back1[c], back1_in[c], b1s.at[c], b1r.at[c])
 
     loads[3].wait()
 
     def pass_back(c):
-        by_row.arrived(back1.at[c], back1_in.at[c], b1s.at[c], b1r.at[c])
-        turned = dot(turn, back1_in[c]).astype(BF16)
-        for t in range(3):
-            back2[c, :, t * 256 : t * 256 + 128] = turned[:N, t * 128 : (t + 1) * 128]
-            back2[c, :, t * 256 + 128 : (t + 1) * 256] = turned[N:, t * 128 : (t + 1) * 128]
-        by_col.start(back2.at[c], back_in.at[c], b2s.at[c], b2r.at[c])
+        by_row.arrived(back1[c], back1_in[c], b1s.at[c], b1r.at[c])
+        turned = dot(turn, back1_in[c][...]).astype(BF16)
+        for t in range(BACK_TILES[c]):
+            back2[c][:, t * 256 : t * 256 + 128] = turned[:N, t * 128 : (t + 1) * 128]
+            back2[c][:, t * 256 + 128 : (t + 1) * 256] = turned[N:, t * 128 : (t + 1) * 128]
+        by_col.start(back2[c], back_in[c], b2s.at[c], b2r.at[c])
 
     def masked(source, g, masks):
         return jnp.concatenate(
@@ -345,38 +352,49 @@
             axis=0,
         )
 
+    pair_id = jnp.floor(local_id * 0.5)
+    second = local_id != pair_id * 2.0
+
     def masks_of(k):
-        return [one_zero(local_id == (OCTET * k + i).astype(F32)) for i in range(OCTET)]
+        return [one_zero(pair_id == (PAIRS * k + i).astype(F32)) for i in range(PAIRS)]
 
     def add_heads(target, g, value):
         for h in range(GROUP):
-            at = (g * GROUP + h) * DH
-            target[:, at : at + DH] += value[h * N : (h + 1) * N]
-
-    def score_octet(k, carry):
+            at = (g * GROUP + h) * 2 * DH
+            target[:, at : at + 2 * DH] += value[h * N : (h + 1) * N]
+
+    def blocks_of(k, kind, g, side, axis):
+        return jnp.concatenate(
+            [blocks_v[2 * (PAIRS * k + i) + side, kind, g] for i in range(PAIRS)], axis=axis
+        )
+
+    def score_step(k, carry):
         masks = masks_of(k)
         for g in range(2):
-            keys = jnp.concatenate([blocks_v[OCTET * k + i, 0, g] for i in range(OCTET)], axis=1)
+            keys = jnp.concatenate([blocks_of(k, 0, g, side, 1) for side in range(2)], axis=0)
             add_heads(score, g, dot_t(masked(heads_v, g, masks), keys))
         return carry
 
-    def value_octet(k, carry):
+    def value_step(k, carry):
         masks = masks_of(k)
         for g in range(2):
-            values = jnp.concatenate([blocks_v[OCTET * k + i, 1, g] for i in range(OCTET)], axis=0)
+            values = jnp.concatenate([blocks_of(k, 1, g, side, 0) for side in range(2)], axis=1)
             add_heads(total, g, dot(masked(prob, g, masks), values))
         return carry
 
-    lax.fori_loop(0, 2, score_octet, 0)
+    def side_of(source, i):
+        at = i * 2 * DH
+        return jnp.where(second, source[:, at + DH : at + 2 * DH], source[:, at : at + DH])
+
+    lax.fori_loop(0, 1, score_step, 0)
     pass_back(0)
-    lax.fori_loop(2, 4, score_octet, 0)
+    lax.fori_loop(1, 2, score_step, 0)
     pass_back(1)
 
     for g in range(2):
         stats = jnp.zeros((N, N), F32)
         for h in range(GROUP):
-            at = (g * GROUP + h) * DH
-            s = score[:, at : at + DH] * SCORE_SCALE
+            s = side_of(score, g * GROUP + h) * SCORE_SCALE
             top = jnp.max(s, axis=1, keepdims=True)
             e = jnp.exp2(s - top)
             prob[g * GROUP + h] = e.astype(BF16)
@@ -384,9 +402,9 @@
             stats = jnp.where(along == 8 + h, jnp.sum(e, axis=1, keepdims=True), stats)
         stat[g] = stats
 
-    lax.fori_loop(0, 2, value_octet, 0)
+    lax.fori_loop(0, 1, value_step, 0)
     pass_back(2)
-    lax.fori_loop(2, 4, value_octet, 0)
+    lax.fori_loop(1, 2, value_step, 0)
 
     for c in range(SHARE_CHUNKS):
         for b in range(4):
@@ -395,8 +413,7 @@
             for g in range(2):
                 stats = stat[g]
                 if h < GROUP:
-                    at = (g * GROUP + h) * DH
-                    sides.append(total[:, at : at + DH] / stats[:, 8 + h : 9 + h])
+                    sides.append(side_of(total, g * GROUP + h) / stats[:, 8 + h : 9 + h])
                 else:
                     high = stats.astype(BF16).astype(F32)
                     rest = stats - high
@@ -408,18 +425,20 @@
             share1[c, :, b * 128 : (b + 1) * 128] = pair_rows(sides[0], sides[1]).astype(BF16)
         by_row.start(share1.at[c], share1_in.at[c], s1s.at[c], s1r.at[c])
 
-    for c in range(BACK_CHUNKS):
-        by_col.arrived(back2.at[c], back_in.at[c], b2s.at[c], b2r.at[c])
-        own = dot(unsort, back_in[c]).astype(BF16)
-        for t in range(3):
-            n = c * 3 + t
+    def take_back(c):
+        by_col.arrived(back2[c], back_in[c], b2s.at[c], b2r.at[c])
+        own = dot(unsort, back_in[c][...]).astype(BF16)
+        for t in range(BACK_TILES[c]):
+            n = BACK_STARTS[c] + t
             if n < GROUP:
                 for half in range(2):
                     store_query(2 * n + half, slice(0, DH), own[:, t * 256 + half * 128 :][:, :DH])
             else:
-                kv_ref[:, (n - GROUP) * 256 : (n - GROUP + 1) * 256] = own[
+                kv_v[:, (n - GROUP) * 256 : (n - GROUP + 1) * 256] = own[
                     :, t * 256 : (t + 1) * 256
                 ]
+
+    take_back(0)
     loads[4].wait()
     spans = [slice(k, k + KEYS) for k in range(0, prefix_v.shape[2], KEYS)]
     ones = jnp.ones((KEYS, DH), BF16)
@@ -458,7 +477,8 @@
     for span in spans:
         first_top = near_scores(query_v[0], 0, span, first_top)
     keep_top(0, first_top)
-    lax.fori_loop(0, TILES // 2, tile, 0)
+    lax.fori_loop(0, 1, tile, 0)
+    take_back(1)
 
     for c in range(SHARE_CHUNKS):
         by_row.arrived(share1.at[c], share1_in.at[c], s1s.at[c], s1r.at[c])
@@ -467,7 +487,10 @@
         share2[c, :, 512:] = turned[N:]
         by_col.start(share2.at[c], share_in.at[c], s2s.at[c], s2r.at[c])
 
-    lax.fori_loop(TILES // 2, TILES - 1, tile, 0)
+    lax.fori_loop(1, TILES - 1, tile, 0)
+    take_back(2)
+    save_kv = pltpu.make_async_copy(kv_v, kv_ref, save_sem.at[2])
+    save_kv.start()
     last_top = near_top[TILES - 1][:, :1]
     last_sums = jnp.zeros((TILE, 2 * DH), F32)
     for span in spans:
@@ -476,6 +499,7 @@
 
     for c in range(SHARE_CHUNKS):
         by_col.arrived(share2.at[c], share_in.at[c], s2s.at[c], s2r.at[c])
+    saves = [save_kv]
     for g in range(2):
         packed = dot(unsort, share_in[1, :, g * 512 + 384 : g * 512 + 512])
         stats = (
@@ -496,21 +520,41 @@
             far = jnp.exp2(top_far - top) * mass_far
             sums = jnp.concatenate([near_total[2 * g, rows], near_total[2 * g + 1, rows]], axis=0)
             whole = sums[:, DH:] * near + far
-            context_ref[:, i * DH : (i + 1) * DH] = (
+            context_v[:, i * DH : (i + 1) * DH] = (
                 (sums[:, :DH] * near + part * far) / whole
             ).astype(BF16)
+
+        lanes = pl.ds(g * GROUP * DH, GROUP * DH)
+        save = pltpu.make_async_copy(
+            context_v.at[:, lanes], context_ref.at[:, lanes], save_sem.at[g]
+        )
+        save.start()
+        saves.append(save)
 
     by_col.sent(id_out1, id_in1, i1s, i1r)
     by_row8.sent(id_out2, id_in2, i2s, i2r)
     for c in range(DELTA_CHUNKS):
-        by_col.sent(out1.at[c], in1.at[c], d1s.at[c], d1r.at[c])
-        by_row.sent(out2.at[c], in2.at[c], d2s.at[c], d2r.at[c])
+        by_col.sent(out1[c], in1[c], d1s.at[c], d1r.at[c])
+        by_row.sent(out2[c], in2[c], d2s.at[c], d2r.at[c])
     for c in range(BACK_CHUNKS):
-        by_row.sent(back1.at[c], back1_in.at[c], b1s.at[c], b1r.at[c])
-        by_col.sent(back2.at[c], back_in.at[c], b2s.at[c], b2r.at[c])
+        by_row.sent(back1[c], back1_in[c], b1s.at[c], b1r.at[c])
+        by_col.sent(back2[c], back_in[c], b2s.at[c], b2r.at[c])
     for c in range(SHARE_CHUNKS):
         by_row.sent(share1.at[c], share1_in.at[c], s1s.at[c], s1r.at[c])
         by_col.sent(share2.at[c], share_in.at[c], s2s.at[c], s2r.at[c])
+    for save in saves:
+        save.wait()
+
+
+def result_kernel(context_in, kv_in, context_ref, kv_ref, sem):
+    copies = [
+        pltpu.make_async_copy(context_in, context_ref, sem.at[0]),
+        pltpu.make_async_copy(kv_in, kv_ref, sem.at[1]),
+    ]
+    for copy in copies:
+        copy.start()
+    for copy in copies:
+        copy.wait()
 
 
 def local(
@@ -530,41 +574,41 @@
     ids = child_parent.reshape(1, N)
     lens = prefix_len.reshape(1, N)
     tokens = prefix_cache.shape[3]
-    back_shape = (BACK_CHUNKS, N, 768)
     share_shape = (SHARE_CHUNKS, N, 1024)
-    return pl.pallas_call(
+    results = (
+        jax.ShapeDtypeStruct((N, HEADS * DH), BF16),
+        jax.ShapeDtypeStruct((N, 512), BF16),
+    )
+    context, new_kv = pl.pallas_call(
         layer_kernel,
         name="decode_layer",
-        out_shape=(
-            jax.ShapeDtypeStruct((N, HEADS * DH), BF16),
-            jax.ShapeDtypeStruct((N, 512), BF16),
-        ),
+        out_shape=results,
         in_specs=[vmem, vmem, vmem, hbm, hbm, hbm, hbm, hbm, hbm],
-        out_specs=(vmem, vmem),
+        out_specs=(hbm, hbm),
         scratch_shapes=[
             pltpu.VMEM((N, D), BF16),
             pltpu.VMEM((PARENTS, D), BF16),
             pltpu.VMEM((PARENTS, 2, 2, BLOCK, DH), BF16),
             pltpu.VMEM((D, 2304), BF16),
-            pltpu.VMEM((DELTA_CHUNKS, N, CHUNK), BF16),
-            pltpu.VMEM((DELTA_CHUNKS, N, CHUNK), BF16),
-            pltpu.VMEM((DELTA_CHUNKS, 2 * N, HALF), BF16),
-            pltpu.VMEM((DELTA_CHUNKS, 2 * N, HALF), BF16),
+            [pltpu.VMEM((N, 2 * half), BF16) for half in DELTA_HALVES],
+            [pltpu.VMEM((N, 2 * half), BF16) for half in DELTA_HALVES],
+            [pltpu.VMEM((2 * N, half), BF16) for half in DELTA_HALVES],
+            [pltpu.VMEM((2 * N, half), BF16) for half in DELTA_HALVES],
             pltpu.VMEM((N, N), BF16),
             pltpu.VMEM((N, N), BF16),
             pltpu.VMEM((N, N), F32),
             pltpu.VMEM((N, N), F32),
             pltpu.VMEM((N, D), BF16),
             pltpu.VMEM((18, N, 128), BF16),
-            pltpu.VMEM((BACK_CHUNKS, 2 * N, 384), BF16),
-            pltpu.VMEM((BACK_CHUNKS, 2 * N, 384), BF16),
-            pltpu.VMEM(back_shape, BF16),
+            [pltpu.VMEM((2 * N, tiles * 128), BF16) for tiles in BACK_TILES],
+            [pltpu.VMEM((2 * N, tiles * 128), BF16) for tiles in BACK_TILES],
+            [pltpu.VMEM((N, tiles * 256), BF16) for tiles in BACK_TILES],
             pltpu.VMEM((HEADS, N, BLOCK), BF16),
             pltpu.VMEM((2, N, N), F32),
             pltpu.VMEM((SHARE_CHUNKS, 2 * N, 512), BF16),
             pltpu.VMEM((SHARE_CHUNKS, 2 * N, 512), BF16),
             pltpu.VMEM(share_shape, BF16),
-            pltpu.VMEM(back_shape, BF16),
+            [pltpu.VMEM((N, tiles * 256), BF16) for tiles in BACK_TILES],
             pltpu.VMEM(share_shape, BF16),
             pltpu.VMEM((2, 2, tokens, DH), BF16),
             pltpu.VMEM((tokens, BLOCK), BF16),
@@ -572,6 +616,9 @@
             pltpu.VMEM((TILE, tokens), F32),
             pltpu.VMEM((TILES, TILE, 2 * DH), F32),
             pltpu.VMEM((TILES, TILE, DH), F32),
+            pltpu.VMEM((N, 512), BF16),
+            pltpu.VMEM((N, HEADS * DH), BF16),
+            dma((3,)),
             dma((6,)),
             dma((DELTA_CHUNKS, COLS)),
             dma((DELTA_CHUNKS, COLS)),
@@ -604,6 +651,15 @@
         w_kv,
         prefix_cache.reshape(prefix_cache.shape[1:]),
     )
+    return pl.pallas_call(
+        result_kernel,
+        name="results",
+        out_shape=results,
+        in_specs=[hbm, hbm],
+        out_specs=(hbm, hbm),
+        scratch_shapes=[dma((2,))],
+        compiler_params=pltpu.CompilerParams(vmem_limit_bytes=60 << 20),
+    )(context, new_kv)
 
 
 def solution(mesh):

time: 78.5 us -> 86.3 us (1.099)
  the two profiles are of different devices: /device:TPU:9 before, /device:TPU:0 now
where the time goes in v4:
time: 86.3 us; the launch traced here: 86.1 us
  Pallas kernels  85.3 us (99%)
    pallas_call x1, Pallas kernels, local(): pl.pallas_call(layer_kernel, name='decode_layer', out_shape=results, in_s...  66.3 us
    pallas_call x1, Pallas kernels, local(): pl.pallas_call(result_kernel, name='results', out_shape=results, in_specs...  19 us

profile of v4, /device:TPU:0, one launch (start us, length us, event | category | flops | bytes accessed | tf_op | source)
XLA Modules:
  0.0 86.1 jit_solution(12719325984689143736)
XLA Ops:
  0.6 66.3 %decode_layer.1 = (bf16[128,1792]{1,0:T(8,128)(2,1)}, bf16[128,512]{1,0:T(8,128)(2,1)}) custom-call(s32[1,128]{1,0:T(1,128)} %bitcast.6, s32[1,128]{1,0:T(1,128)} %bitcast.7, f32[28,128]{1,0:T(8,128)} %bitcast.5, bf16[128,3584]{1,0:T(8,128)(2,1)} %delta_hbm.1, bf16[32,3584]{1,0:T(8,128)(2,1)} %hidden_hbm.1, bf16[32,2,2,128,128]{4,3,2,1,0:T(8,128)(2,1)} %blocks_hbm.1, ...), custom_call_target="tpu_custom_call" | custom-call | tf_op jit(solution)/shard_map/decode_layer/pallas_call | solution.py:582
  67.0 19.0 %results.1 = (bf16[128,1792]{1,0:T(8,128)(2,1)}, bf16[128,512]{1,0:T(8,128)(2,1)}) custom-call(bf16[128,1792]{1,0:T(8,128)(2,1)} %get-tuple-element.4.context_in, bf16[128,512]{1,0:T(8,128)(2,1)} %get-tuple-element.5.kv_in), custom_call_target="tpu_custom_call" | custom-call | tf_op jit(solution)/shard_map/results/pallas_call | solution.py:654

commit v5 on v4

--- a/solution.py
+++ b/solution.py
@@ -546,15 +546,22 @@
         save.wait()
 
 
-def result_kernel(context_in, kv_in, context_ref, kv_ref, sem):
-    copies = [
-        pltpu.make_async_copy(context_in, context_ref, sem.at[0]),
-        pltpu.make_async_copy(kv_in, kv_ref, sem.at[1]),
+def result_kernel(context_in, kv_in, context_ref, kv_ref, context_v, kv_v, sem):
+    top, bottom = pl.ds(0, SIDE), pl.ds(SIDE, SIDE)
+    hops = [
+        (context_in.at[top], context_v.at[top], context_ref.at[top]),
+        (context_in.at[bottom], context_v.at[bottom], context_ref.at[bottom]),
+        (kv_in, kv_v, kv_ref),
     ]
-    for copy in copies:
-        copy.start()
-    for copy in copies:
-        copy.wait()
+    fetches = [pltpu.make_async_copy(h[0], h[1], sem.at[0, i]) for i, h in enumerate(hops)]
+    stores = [pltpu.make_async_copy(h[1], h[2], sem.at[1, i]) for i, h in enumerate(hops)]
+    for fetch in fetches:
+        fetch.start()
+    for fetch, store in zip(fetches, stores):
+        fetch.wait()
+        store.start()
+    for store in stores:
+        store.wait()
 
 
 def local(
@@ -657,7 +664,11 @@
         out_shape=results,
         in_specs=[hbm, hbm],
         out_specs=(hbm, hbm),
-        scratch_shapes=[dma((2,))],
+        scratch_shapes=[
+            pltpu.VMEM((N, HEADS * DH), BF16),
+            pltpu.VMEM((N, 512), BF16),
+            dma((2, 3)),
+        ],
         compiler_params=pltpu.CompilerParams(vmem_limit_bytes=60 << 20),
     )(context, new_kv)
 

time: 86.3 us -> 69.2 us (0.80)
  Pallas kernels: 85.3 us -> 68.2 us
    pallas_call x1, Pallas kernels: 19 us -> 1.83 us  [local(): pl.pallas_call(result_kernel, name='results', out_shape=results, in_specs...]
where the time goes in v5:
time: 69.2 us; the launch traced here: 69 us
  Pallas kernels  68.2 us (99%)
  between operations  0.8 us (1%)
    pallas_call x1, Pallas kernels, local(): pl.pallas_call(layer_kernel, name='decode_layer', out_shape=results, in_s...  66.3 us
    pallas_call x1, Pallas kernels, local(): pl.pallas_call(result_kernel, name='results', out_shape=results, in_specs...  1.83 us

profile of v5, /device:TPU:0, one launch (start us, length us, event | category | flops | bytes accessed | tf_op | source)
XLA Modules:
  0.0 69.0 jit_solution(13312066344483747787)
XLA Ops:
  0.6 66.3 %decode_layer.1 = (bf16[128,1792]{1,0:T(8,128)(2,1)}, bf16[128,512]{1,0:T(8,128)(2,1)}) custom-call(s32[1,128]{1,0:T(1,128)} %bitcast.6, s32[1,128]{1,0:T(1,128)} %bitcast.7, f32[28,128]{1,0:T(8,128)} %bitcast.5, bf16[128,3584]{1,0:T(8,128)(2,1)} %delta_hbm.1, bf16[32,3584]{1,0:T(8,128)(2,1)} %hidden_hbm.1, bf16[32,2,2,128,128]{4,3,2,1,0:T(8,128)(2,1)} %blocks_hbm.1, ...), custom_call_target="tpu_custom_call" | custom-call | tf_op jit(solution)/shard_map/decode_layer/pallas_call | solution.py:589
  67.0 1.8 %results.1 = (bf16[128,1792]{1,0:T(8,128)(2,1)}, bf16[128,512]{1,0:T(8,128)(2,1)}) custom-call(bf16[128,1792]{1,0:T(8,128)(2,1)} %get-tuple-element.4.context_in, bf16[128,512]{1,0:T(8,128)(2,1)} %get-tuple-element.5.kv_in), custom_call_target="tpu_custom_call" | custom-call | tf_op jit(solution)/shard_map/results/pallas_call | solution.py:661

commit v6 on v5

--- a/solution.py
+++ b/solution.py
@@ -92,29 +92,37 @@
         return pltpu.make_async_remote_copy(
             src_ref=self.part(src, k),
             dst_ref=self.part(dst, slot),
-            send_sem=send.at[k],
-            recv_sem=recv.at[slot],
+            send_sem=send,
+            recv_sem=recv,
             device_id={self.axis: k},
             device_id_type=pl.DeviceIdType.MESH,
         )
 
-    def each(self, act):
+    def whole(self, src, dst, send, recv):
+        rows = pl.ds(0, (self.count - 1) * self.rows)
+        return pltpu.make_async_remote_copy(
+            src_ref=src.at[rows],
+            dst_ref=dst.at[rows],
+            send_sem=send,
+            recv_sem=recv,
+            device_id={self.axis: lax.rem(self.me + 1, self.count)},
+            device_id_type=pl.DeviceIdType.MESH,
+        )
+
+    def start(self, src, dst, send, recv):
         def body(k, carry):
-            act(lax.rem(self.me + k, self.count))
+            self.copy(src, dst, send, recv, lax.rem(self.me + k, self.count), self.me).start()
             return carry
 
         lax.fori_loop(1, self.count, body, 0)
-
-    def start(self, src, dst, send, recv):
-        self.each(lambda k: self.copy(src, dst, send, recv, k, self.me).start())
         own = pl.ds(pl.multiple_of(self.me * self.rows, self.rows), self.rows)
         dst[own, :] = src[own, :]
 
     def arrived(self, src, dst, send, recv):
-        self.each(lambda k: self.copy(src, dst, send, recv, k, k).wait_recv())
+        self.whole(src, dst, send, recv).wait_recv()
 
     def sent(self, src, dst, send, recv):
-        self.each(lambda k: self.copy(src, dst, send, recv, k, self.me).wait_send())
+        self.whole(src, dst, send, recv).wait_send()
 
 
 def layer_kernel(
@@ -627,22 +635,22 @@
             pltpu.VMEM((N, HEADS * DH), BF16),
             dma((3,)),
             dma((6,)),
-            dma((DELTA_CHUNKS, COLS)),
-            dma((DELTA_CHUNKS, COLS)),
-            dma((DELTA_CHUNKS, ROWS)),
-            dma((DELTA_CHUNKS, ROWS)),
-            dma((COLS,)),
-            dma((COLS,)),
-            dma((ROWS,)),
-            dma((ROWS,)),
-            dma((BACK_CHUNKS, ROWS)),
-            dma((BACK_CHUNKS, ROWS)),
-            dma((BACK_CHUNKS, COLS)),
-            dma((BACK_CHUNKS, COLS)),
-            dma((SHARE_CHUNKS, ROWS)),
-            dma((SHARE_CHUNKS, ROWS)),
-            dma((SHARE_CHUNKS, COLS)),
-            dma((SHARE_CHUNKS, COLS)),
+            dma((DELTA_CHUNKS,)),
+            dma((DELTA_CHUNKS,)),
+            dma((DELTA_CHUNKS,)),
+            dma((DELTA_CHUNKS,)),
+            dma(()),
+            dma(()),
+            dma(()),
+            dma(()),
+            dma((BACK_CHUNKS,)),
+            dma((BACK_CHUNKS,)),
+            dma((BACK_CHUNKS,)),
+            dma((BACK_CHUNKS,)),
+            dma((SHARE_CHUNKS,)),
+            dma((SHARE_CHUNKS,)),
+            dma((SHARE_CHUNKS,)),
+            dma((SHARE_CHUNKS,)),
         ],
         compiler_params=pltpu.CompilerParams(
             collective_id=0, has_side_effects=True, vmem_limit_bytes=60 << 20

time: 69.2 us -> 63.5 us (0.918)
  Pallas kernels: 68.2 us -> 62.4 us
    pallas_call x1, Pallas kernels: 66.3 us -> 60.6 us  [local(): pl.pallas_call(layer_kernel, name='decode_layer', out_shape=results, in_s...]
where the time goes in v6:
time: 63.5 us; the launch traced here: 63.2 us
  Pallas kernels  62.4 us (98%)
  between operations  0.8 us (1%)
    pallas_call x1, Pallas kernels, local(): pl.pallas_call(layer_kernel, name='decode_layer', out_shape=results, in_s...  60.6 us
    pallas_call x1, Pallas kernels, local(): pl.pallas_call(result_kernel, name='results', out_shape=results, in_specs...  1.83 us

profile of v6, /device:TPU:0, one launch (start us, length us, event | category | flops | bytes accessed | tf_op | source)
XLA Modules:
  0.0 63.2 jit_solution(8564644199826897179)
XLA Ops:
  0.6 60.6 %decode_layer.1 = (bf16[128,1792]{1,0:T(8,128)(2,1)}, bf16[128,512]{1,0:T(8,128)(2,1)}) custom-call(s32[1,128]{1,0:T(1,128)} %bitcast.6, s32[1,128]{1,0:T(1,128)} %bitcast.7, f32[28,128]{1,0:T(8,128)} %bitcast.5, bf16[128,3584]{1,0:T(8,128)(2,1)} %delta_hbm.1, bf16[32,3584]{1,0:T(8,128)(2,1)} %hidden_hbm.1, bf16[32,2,2,128,128]{4,3,2,1,0:T(8,128)(2,1)} %blocks_hbm.1, ...), custom_call_target="tpu_custom_call" | custom-call | tf_op jit(solution)/shard_map/decode_layer/pallas_call | solution.py:597
  61.2 1.8 %results.1 = (bf16[128,1792]{1,0:T(8,128)(2,1)}, bf16[128,512]{1,0:T(8,128)(2,1)}) custom-call(bf16[128,1792]{1,0:T(8,128)(2,1)} %get-tuple-element.4.context_in, bf16[128,512]{1,0:T(8,128)(2,1)} %get-tuple-element.5.kv_in), custom_call_target="tpu_custom_call" | custom-call | tf_op jit(solution)/shard_map/results/pallas_call | solution.py:669

commit v7 on v6

--- a/solution.py
+++ b/solution.py
@@ -410,9 +410,7 @@
             stats = jnp.where(along == 8 + h, jnp.sum(e, axis=1, keepdims=True), stats)
         stat[g] = stats
 
-    lax.fori_loop(0, 1, value_step, 0)
-    pass_back(2)
-    lax.fori_loop(1, 2, value_step, 0)
+    lax.fori_loop(0, 2, value_step, 0)
 
     for c in range(SHARE_CHUNKS):
         for b in range(4):
@@ -485,6 +483,7 @@
     for span in spans:
         first_top = near_scores(query_v[0], 0, span, first_top)
     keep_top(0, first_top)
+    pass_back(2)
     lax.fori_loop(0, 1, tile, 0)
     take_back(1)
 

time: 63.5 us -> 64.3 us (1.013)
  Pallas kernels: 62.4 us -> 63.3 us
    pallas_call x1, Pallas kernels: 60.6 us -> 61.5 us  [local(): pl.pallas_call(layer_kernel, name='decode_layer', out_shape=results, in_s...]
where the time goes in v7:
time: 64.3 us; the launch traced here: 64.1 us
  Pallas kernels  63.3 us (98%)
  between operations  0.8 us (1%)
    pallas_call x1, Pallas kernels, local(): pl.pallas_call(layer_kernel, name='decode_layer', out_shape=results, in_s...  61.5 us
    pallas_call x1, Pallas kernels, local(): pl.pallas_call(result_kernel, name='results', out_shape=results, in_specs...  1.83 us

profile of v7, /device:TPU:0, one launch (start us, length us, event | category | flops | bytes accessed | tf_op | source)
XLA Modules:
  0.0 64.1 jit_solution(16566048181129077996)
XLA Ops:
  0.6 61.5 %decode_layer.1 = (bf16[128,1792]{1,0:T(8,128)(2,1)}, bf16[128,512]{1,0:T(8,128)(2,1)}) custom-call(s32[1,128]{1,0:T(1,128)} %bitcast.6, s32[1,128]{1,0:T(1,128)} %bitcast.7, f32[28,128]{1,0:T(8,128)} %bitcast.5, bf16[128,3584]{1,0:T(8,128)(2,1)} %delta_hbm.1, bf16[32,3584]{1,0:T(8,128)(2,1)} %hidden_hbm.1, bf16[32,2,2,128,128]{4,3,2,1,0:T(8,128)(2,1)} %blocks_hbm.1, ...), custom_call_target="tpu_custom_call" | custom-call | tf_op jit(solution)/shard_map/decode_layer/pallas_call | solution.py:596
  62.1 1.8 %results.1 = (bf16[128,1792]{1,0:T(8,128)(2,1)}, bf16[128,512]{1,0:T(8,128)(2,1)}) custom-call(bf16[128,1792]{1,0:T(8,128)(2,1)} %get-tuple-element.4.context_in, bf16[128,512]{1,0:T(8,128)(2,1)} %get-tuple-element.5.kv_in), custom_call_target="tpu_custom_call" | custom-call | tf_op jit(solution)/shard_map/results/pallas_call | solution.py:668
